TPU v7x, 256 devices: a whole 4x4x8 slice. The times are simulated.
256 devices in a mesh: seq: 64 (over z_lo, y, x, core), ch: 4 (over z_hi).
Axes of the slice: x: 4, y: 4, z: 8 (z_hi: 4, z_lo: 2; z = z_hi * 2 + z_lo), core: 2. Of those that a mesh axis runs over, the one named last changes fastest.
Arguments:
- inputs: bfloat16 [256, 32768], P('ch', 'seq'), may hold values from -6 to 6
- w_value: bfloat16 [256, 256], P(None, 'ch'), may hold values from -0.375 to 0.375
- w_gate: bfloat16 [256, 256], P(None, 'ch'), may hold values from -0.375 to 0.375
- w_out: bfloat16 [256, 256], P('ch'), may hold values from -0.375 to 0.375
- filter_taps: float32 [256, 32768], P('ch', 'seq'), may hold values from -6 to 6
- grad_out: bfloat16 [256, 32768], P('ch', 'seq'), may hold values from -6 to 6
Outputs:
- d_inputs: bfloat16 [256, 32768], P('ch', 'seq')
- d_w_value: float32 [256, 256], P(None, 'ch')
- d_w_gate: float32 [256, 256], P(None, 'ch')
- d_w_out: float32 [256, 256], P('ch')
- d_filter: float32 [256, 32768], P('ch', 'seq')
All inputs are finite; a program needn't handle non-finite values.
Results may differ from a plain program's by a relative error of at most 0.015.
Values may be sent and summed in bfloat16 or wider, within the bound.
No kernel may reach another device: no remote copies, remote signals or barrier semaphores. Data moves between devices by JAX's collectives and lax.ppermute only.
A program may use at most 64 MiB of HBM per device.

v0:
```python
import math

import jax
import jax.numpy as jnp
import ml_dtypes
import numpy as np
from jax import lax
from jax.experimental import pallas as pl
from jax.experimental.pallas import tpu as pltpu
from jax.sharding import PartitionSpec as P

F32 = jnp.float32
BF16 = jnp.bfloat16
LANES = 128
GROUP = 16


def halves(table):
    high = table.astype(ml_dtypes.bfloat16)
    low = (table - high.astype(np.float64)).astype(ml_dtypes.bfloat16)
    return high, low


def transform_tables(tokens):
    rows = tokens // LANES
    length = 2 * tokens
    per_sender = rows // 64
    order = np.arange(rows).reshape(64 // GROUP, GROUP, per_sender)
    order = order.transpose(0, 2, 1).reshape(-1)
    k1 = np.arange(rows) + 0.5
    theta = 2.0 * np.pi * ((k1[:, None] * order[None, :]) % (2 * rows)) / (2 * rows)
    outer = np.concatenate([np.cos(theta), -np.sin(theta)], axis=0)
    q = np.arange(LANES)
    phi = 2.0 * np.pi * ((q[:, None] * q[None, :]) % LANES) / LANES
    c, s = np.cos(phi), np.sin(phi)
    inner = np.block([[c, -s], [s, c]])
    twist = 2.0 * np.pi * k1[:, None] * q[None, :] / length
    twiddle = np.stack([np.cos(twist), -np.sin(twist)]).astype(np.float32)
    scale = 2.0 / length
    return halves(outer) + halves(inner) + halves(inner.T) + halves(outer.T * scale) + (twiddle,)


def exchange_table():
    table = np.zeros((GROUP * GROUP, GROUP * GROUP), np.float32)
    for a in range(GROUP):
        for b in range(GROUP):
            table[a * GROUP + b, b * GROUP + a] = 1.0
    return table.astype(ml_dtypes.bfloat16)


def dot(left, right, dims=((1,), (0,))):
    return lax.dot_general(left, right, (dims, ((), ())), preferred_element_type=F32)


def split_up(value):
    high = value.astype(BF16)
    return high, (value - high.astype(F32)).astype(BF16)


def dot3_left(table_high, table_low, value):
    high, low = split_up(value)
    return dot(table_high, high) + (dot(table_high, low) + dot(table_low, high))


def dot3_right(value, table_high, table_low):
    high, low = split_up(value)
    return dot(high, table_high) + (dot(low, table_high) + dot(high, table_low))


def write_messages(out_ref, swap, parts):
    for g in range(64 // GROUP):
        rows = jnp.concatenate([x[g * GROUP : (g + 1) * GROUP] for x in parts], axis=0)
        out_ref[g * GROUP * GROUP : (g + 1) * GROUP * GROUP, :] = dot(swap, rows).astype(BF16)


def read_messages(in_ref, swap):
    size = GROUP * GROUP
    return [
        dot(swap, in_ref[g * size : (g + 1) * size, :]).astype(BF16) for g in range(64 // GROUP)
    ]


def lane_blocks(value):
    return [value[:, u * LANES : (u + 1) * LANES] for u in range(value.shape[1] // LANES)]


def project_kernel(
    ch_ref, own_ref, got1_ref, got3_ref, got2_ref, wv_ref, wg_ref, wo_ref, taps_ref, swap_ref,
    msg_ref, gate_ref, dgated_ref, in_ref, grad_ref,
):
    ch = ch_ref[0]
    for shift, ref in ((0, own_ref), (1, got1_ref), (3, got3_ref), (2, got2_ref)):
        at = pl.multiple_of(lax.rem(ch + (4 - shift), 4) * 64, 64)
        in_ref[pl.ds(at, 64), :] = ref[:64, :]
        grad_ref[pl.ds(at, 64), :] = ref[64:, :]
    full_in = in_ref[...]
    value = dot(wv_ref[...], full_in).astype(BF16)
    gate = dot(wg_ref[...], full_in)
    d_gated = dot(wo_ref[...], grad_ref[...])
    gate_ref[...] = gate
    dgated_ref[...] = d_gated
    d_mixed = (d_gated * gate).astype(BF16)
    tap_high, tap_low = split_up(taps_ref[...])
    parts = []
    for x in (value, d_mixed, tap_high, tap_low):
        parts += lane_blocks(x)
    write_messages(msg_ref, swap_ref[...], parts)


def convolve_kernel(
    got_ref, swap_ref, oh_ref, ol_ref, ih_ref, il_ref, jh_ref, jl_ref, ph_ref, pl_ref, tw_ref,
    out_ref,
):
    swap = swap_ref[...]
    groups = read_messages(got_ref, swap)

    def signal(k):
        return jnp.concatenate([x[k * 64 : (k + 1) * 64] for x in groups], axis=0)

    data = jnp.concatenate([signal(k) for k in range(4)], axis=1)
    first = dot(oh_ref[...], data) + dot(ol_ref[...], data)
    half = first.shape[0] // 2
    tw_re, tw_im = tw_ref[0], tw_ref[1]

    def column(k):
        return first[:, k * LANES : (k + 1) * LANES]

    spectra = []
    for a in (column(0), column(1), column(2) + column(3)):
        re, im = a[:half], a[half:]
        z = jnp.concatenate([re * tw_re - im * tw_im, re * tw_im + im * tw_re], axis=1)
        x = dot3_right(z, ih_ref[...], il_ref[...])
        spectra.append((x[:, :LANES], x[:, LANES:]))
    (v_re, v_im), (d_re, d_im), (h_re, h_im) = spectra
    products = (
        (h_re * v_re - h_im * v_im, h_re * v_im + h_im * v_re),
        (h_re * d_re + h_im * d_im, h_re * d_im - h_im * d_re),
        (v_re * d_re + v_im * d_im, v_re * d_im - v_im * d_re),
    )
    back = []
    for re, im in products:
        y = dot3_right(jnp.concatenate([re, im], axis=1), jh_ref[...], jl_ref[...])
        re, im = y[:, :LANES], y[:, LANES:]
        b = jnp.concatenate([re * tw_re + im * tw_im, im * tw_re - re * tw_im], axis=0)
        back.append(dot3_left(ph_ref[...], pl_ref[...], b))
    mixed, d_value, d_filter = back
    filter_high, filter_low = split_up(d_filter)
    size = GROUP * GROUP
    for g in range(64 // GROUP):
        rows = jnp.concatenate(
            [
                x[g * 64 : (g + 1) * 64]
                for x in (mixed.astype(BF16), d_value.astype(BF16), filter_high, filter_low)
            ],
            axis=0,
        )
        out_ref[g * size : (g + 1) * size, :] = dot(swap, rows).astype(BF16)


def gradient_kernel(
    ch_ref, got_ref, swap_ref, gate_ref, dgated_ref, in_ref, grad_ref, wv_ref, wg_ref,
    sums_ref, own_ref, send1_ref, send3_ref, send2_ref, filt_ref, part_ref, *, scale
):
    groups = read_messages(got_ref, swap_ref[...])

    def signal(k):
        cols = []
        for u in range(4):
            at = (k * 4 + u) * GROUP
            cols.append(jnp.concatenate([x[at : at + GROUP] for x in groups], axis=0))
        return jnp.concatenate(cols, axis=1)

    mixed = signal(0).astype(F32)
    d_value = signal(1)
    filt_ref[...] = (signal(2).astype(F32) + signal(3).astype(F32)) * scale
    gated_out = (gate_ref[...] * mixed).astype(BF16)
    d_gate = (dgated_ref[...] * mixed).astype(BF16)
    both = jnp.concatenate([d_value, d_gate], axis=0)
    weights = jnp.concatenate([wv_ref[...], wg_ref[...]], axis=0)
    part_ref[...] = dot(weights, both, ((0,), (0,)))
    ch = ch_ref[0]

    def block(shift):
        at = pl.multiple_of(lax.rem(ch + shift, 4) * 64, 64)
        return part_ref[pl.ds(at, 64), :]

    own_ref[...] = block(0)
    send1_ref[...] = block(1).astype(BF16)
    send3_ref[...] = block(3).astype(BF16)
    send2_ref[...] = block(2).astype(BF16)
    term = dot(both, in_ref[...], ((1,), (1,)))
    out_term = dot(gated_out, grad_ref[...], ((1,), (1,)))
    pieces = lane_blocks(term[:64]) + lane_blocks(term[64:]) + lane_blocks(out_term)
    pieces += [jnp.zeros_like(pieces[0])] * 2
    for r, piece in enumerate(pieces):
        sums_ref[pl.ds(r, 64, stride=8), :] = piece


def total_kernel(got_ref, out_ref, *, scale):
    total = got_ref[...].reshape(64, 8, LANES).sum(axis=0) * scale
    out_ref[...] = jnp.broadcast_to(total[None], (64, 8, LANES)).reshape(512, LANES)


def settle_kernel(got_ref, dwv_ref, dwg_ref, dwo_ref):
    for k, ref in enumerate((dwv_ref, dwg_ref, dwo_ref)):
        ref[...] = jnp.concatenate(
            [got_ref[pl.ds(2 * k + j, 64, stride=8), :] for j in range(2)], axis=1
        )


def shaped(shape, dtype):
    return jax.ShapeDtypeStruct(shape, dtype)


VMEM = pl.BlockSpec(memory_space=pltpu.VMEM)
SMEM = pl.BlockSpec(memory_space=pltpu.SMEM)


def exchanged(rows, axis):
    count = lax.axis_size(axis)
    parts = rows.reshape(count, rows.shape[0] // count, rows.shape[1])
    return lax.all_to_all(parts, axis, 0, 0, tiled=True).reshape(rows.shape)


def shifted(value, shift):
    return lax.ppermute(value, "ch", [(i, (i + shift) % 4) for i in range(4)])


def on_device(inputs, w_value, w_gate, w_out, filter_taps, grad_out):
    tokens = filter_taps.shape[1] * lax.axis_size("seq")
    scale = 1.0 / math.sqrt(tokens)
    tables = [jnp.asarray(t) for t in transform_tables(tokens)]
    swap = jnp.asarray(exchange_table())
    ch = lax.axis_index("ch").astype(jnp.int32).reshape(1)
    wv, wg = w_value.T, w_gate.T

    own = jnp.concatenate([inputs, grad_out], axis=0)
    got = [shifted(own, s) for s in (1, 3, 2)]
    msg, gate, d_gated, full_in, full_grad = pl.pallas_call(
        project_kernel,
        out_shape=(
            shaped((1024, LANES), BF16),
            shaped((64, 512), F32),
            shaped((64, 512), F32),
            shaped((256, 512), BF16),
            shaped((256, 512), BF16),
        ),
        in_specs=[SMEM] + [VMEM] * 9,
        out_specs=[VMEM] * 5,
        name="project",
    )(ch, own, *got, wv, wg, w_out, filter_taps, swap)
    back = pl.pallas_call(
        convolve_kernel,
        out_shape=shaped((1024, LANES), BF16),
        in_specs=[VMEM] * 11,
        out_specs=VMEM,
        name="convolve",
    )(exchanged(msg, "seq"), swap, *tables)
    sums, mine, send1, send3, send2, d_filter = pl.pallas_call(
        lambda *refs: gradient_kernel(*refs, scale=scale),
        out_shape=(
            shaped((512, LANES), F32),
            shaped((64, 512), F32),
            shaped((64, 512), BF16),
            shaped((64, 512), BF16),
            shaped((64, 512), BF16),
            shaped((64, 512), F32),
        ),
        in_specs=[SMEM] + [VMEM] * 8,
        out_specs=[VMEM] * 6,
        scratch_shapes=[pltpu.VMEM((256, 512), F32)],
        name="gradients",
    )(ch, exchanged(back, "seq"), swap, gate, d_gated, full_in, full_grad, wv, wg)
    came = [shifted(x, s) for x, s in ((send1, 1), (send3, 3), (send2, 2))]
    d_inputs = mine
    for x in came:
        d_inputs = d_inputs + x.astype(F32)
    d_inputs = d_inputs.astype(BF16)
    total = pl.pallas_call(
        lambda *refs: total_kernel(*refs, scale=scale),
        out_shape=shaped((512, LANES), F32),
        in_specs=[VMEM],
        out_specs=VMEM,
        name="total",
    )(exchanged(sums, "seq"))
    dwv, dwg, dwo = pl.pallas_call(
        settle_kernel,
        out_shape=(shaped((64, 256), F32),) * 3,
        in_specs=[VMEM],
        out_specs=[VMEM] * 3,
        name="settle",
    )(exchanged(total, "seq"))
    return d_inputs, dwv.T, dwg.T, dwo, d_filter


def solution(mesh):
    placed = (
        P("ch", "seq"),
        P(None, "ch"),
        P(None, "ch"),
        P("ch", None),
        P("ch", "seq"),
        P("ch", "seq"),
    )
    return jax.shard_map(
        on_device,
        mesh=mesh,
        in_specs=placed,
        out_specs=(P("ch", "seq"), P(None, "ch"), P(None, "ch"), P("ch", None), P("ch", "seq")),
        check_vma=False,
    )
```

profile of v0, /device:TPU:32, one launch (start us, length us, event | category | flops | bytes accessed | tf_op | source)
XLA Modules:
  0.0 104.2 jit_solution(6226611701377169408)
XLA Ops:
  0.6 0.0 copy-start.6
  0.6 0.9 constant_dynamic-update-slice_fusion.1
  1.5 0.0 copy-done.6
  1.5 0.0 copy-start.1
  1.5 6.4 %collective-permute-start.2 = (bf16[128,512]{1,0:T(8,128)(2,1)S(1)}, bf16[128,512]{1,0:T(8,128)(2,1)S(1)}, u32[]{:S(2)}, u32[]{:S(2)}) collective-permute-start(bf16[128,512]{1,0:T(8,128)(2,1)S(1)} %constant_dynamic-update-slice_fusion.own_ref), channel_id=1, source_target_pairs={{0,2},{1,3},{2,0},{3,1},{4,6},{5,7},{6,4},{7,5},{8,10},{9,11},{10,... | collective-permute-start | bytes 393224 | tf_op jit(solution)/shard_map/ppermute | solution.py:226
  7.9 0.6 collective-permute-start.1
  8.5 2.4 %collective-permute-start = (bf16[128,512]{1,0:T(8,128)(2,1)S(1)}, bf16[128,512]{1,0:T(8,128)(2,1)S(1)}, u32[]{:S(2)}, u32[]{:S(2)}) collective-permute-start(bf16[128,512]{1,0:T(8,128)(2,1)S(1)} %constant_dynamic-update-slice_fusion.own_ref), channel_id=1, source_target_pairs={{0,1},{1,2},{2,3},{3,0},{4,5},{5,6},{6,7},{7,4},{8,9},{9,10},{10,1... | collective-permute-start | bytes 393224 | tf_op jit(solution)/shard_map/ppermute | solution.py:226
  10.8 4.4 %collective-permute-done.2.got2_ref = bf16[128,512]{1,0:T(8,128)(2,1)S(1)} collective-permute-done((bf16[128,512]{1,0:T(8,128)(2,1)S(1)}, bf16[128,512]{1,0:T(8,128)(2,1)S(1)}, u32[]{:S(2)}, u32[]{:S(2)}) %collective-permute-start.2) | collective-permute-done | bytes 131104 | tf_op jit(solution)/shard_map/ppermute | solution.py:226
  15.3 3.9 %collective-permute-done.1.got3_ref = bf16[128,512]{1,0:T(8,128)(2,1)S(1)} collective-permute-done((bf16[128,512]{1,0:T(8,128)(2,1)S(1)}, bf16[128,512]{1,0:T(8,128)(2,1)S(1)}, u32[]{:S(2)}, u32[]{:S(2)}) %collective-permute-start.1) | collective-permute-done | bytes 131104 | tf_op jit(solution)/shard_map/ppermute | solution.py:226
  19.2 0.6 collective-permute-done.got1_ref
  19.8 0.0 copy-done.1
  19.8 0.1 copy-done.4
  19.8 0.6 copy-done.5
  20.4 2.5 %project.1 = (bf16[1024,128]{1,0:T(8,128)(2,1)}, f32[64,512]{1,0:T(8,128)}, f32[64,512]{1,0:T(8,128)}, bf16[256,512]{1,0:T(8,128)(2,1)}, bf16[256,512]{1,0:T(8,128)(2,1)}) custom-call(s32[1]{0:T(128)} %bitcast.ch_ref.refs_0_, bf16[128,512]{1,0:T(8,128)(2,1)} %copy-done.1, bf16[128,512]{1,0:T(8,128)(2,1)} %copy-done.5, bf16[128,512]{1,0:T(8,128)(2,1)} %copy-done.4, ...), custom_call_target="tpu_custom_call" | custom-call | tf_op jit(solution)/shard_map/project/pallas_call | solution.py:239
  22.9 18.4 %all_to_all.20 = bf16[64,16,128]{2,1,0:T(8,128)(2,1)} all-to-all(bf16[64,16,128]{2,1,0:T(8,128)(2,1)} %bitcast.20), channel_id=1, replica_groups=mesh['seq'=64,'ch'=4] {'seq'}, dimensions={0} | all-to-all | bytes 524288 | tf_op jit(solution)/shard_map/all_to_all | solution.py:222
  41.3 5.6 %convolve.1 = bf16[1024,128]{1,0:T(8,128)(2,1)} custom-call(bf16[1024,128]{1,0:T(8,128)(2,1)} %bitcast.13, bf16[256,256]{1,0:T(8,128)(2,1)} %constant.33.clone.swap_ref.refs_2_, bf16[512,256]{1,0:T(8,128)(2,1)} %constant.24.clone.oh_ref, bf16[512,256]{1,0:T(8,128)(2,1)} %constant.25.clone.ol_ref, bf16[256,256]{1,0:T(8,128)(2,1)} %constant.26.clone.ih_ref, ...), custom_call_target="tpu_custom_call" | custom-call | tf_op jit(solution)/shard_map/convolve/pallas_call | solution.py:252
  46.9 15.0 %all_to_all.21 = bf16[64,16,128]{2,1,0:T(8,128)(2,1)} all-to-all(bf16[64,16,128]{2,1,0:T(8,128)(2,1)} %bitcast.14), channel_id=1, replica_groups=mesh['seq'=64,'ch'=4] {'seq'}, dimensions={0} | all-to-all | bytes 524288 | tf_op jit(solution)/shard_map/all_to_all | solution.py:222
  61.9 2.7 %gradients.1 = (f32[512,128]{1,0:T(8,128)}, f32[64,512]{1,0:T(8,128)}, bf16[64,512]{1,0:T(8,128)(2,1)}, bf16[64,512]{1,0:T(8,128)(2,1)}, bf16[64,512]{1,0:T(8,128)(2,1)}, /*index=5*/f32[64,512]{1,0:T(8,128)}) custom-call(s32[1]{0:T(128)} %bitcast.ch_ref.refs_0_, bf16[1024,128]{1,0:T(8,128)(2,1)} %bitcast.18, ...), custom_call_target="tpu_custom_call" | custom-call | tf_op jit(solution)/shard_map/gradients/pallas_call | solution.py:259
  64.6 15.0 %all_to_all.22 = f32[64,8,128]{2,1,0:T(8,128)} all-to-all(f32[64,8,128]{2,1,0:T(8,128)} %bitcast.19), channel_id=1, replica_groups=mesh['seq'=64,'ch'=4] {'seq'}, dimensions={0} | all-to-all | bytes 524288 | tf_op jit(solution)/shard_map/all_to_all | solution.py:222
  79.6 1.7 %total.1 = f32[512,128]{1,0:T(8,128)} custom-call(f32[512,128]{1,0:T(8,128)} %bitcast.17), custom_call_target="tpu_custom_call" | custom-call | tf_op jit(solution)/shard_map/total/pallas_call | solution.py:279
  81.4 5.4 %all-to-all-start.3 = ((f32[64,8,128]{2,1,0:T(8,128)}), f32[64,8,128]{2,1,0:T(8,128)S(1)}, u32[]{:S(2)}, u32[]{:S(2)}) async-start(f32[64,8,128]{2,1,0:T(8,128)} %bitcast.16), calls=%async_computation.3 | async-start | bytes 524288 | tf_op jit(solution)/shard_map/all_to_all | solution.py:222
  86.8 0.0 copy-done.9
  86.8 2.2 %collective-permute-start.3 = (bf16[64,512]{1,0:T(8,128)(2,1)S(1)}, bf16[64,512]{1,0:T(8,128)(2,1)S(1)}, u32[]{:S(2)}, u32[]{:S(2)}) collective-permute-start(bf16[64,512]{1,0:T(8,128)(2,1)S(1)} %copy-done.9), channel_id=1, source_target_pairs={{0,1},{1,2},{2,3},{3,0},{4,5},{5,6},{6,7},{7,4},{8,9},{9,10},{10,1... | collective-permute-start | bytes 196616 | tf_op jit(solution)/shard_map/ppermute | solution.py:226
  89.0 2.0 %collective-permute-start.4 = (bf16[64,512]{1,0:T(8,128)(2,1)S(1)}, bf16[64,512]{1,0:T(8,128)(2,1)S(1)}, u32[]{:S(2)}, u32[]{:S(2)}) collective-permute-start(bf16[64,512]{1,0:T(8,128)(2,1)S(1)} %copy-done.8), channel_id=1, source_target_pairs={{0,3},{1,0},{2,1},{3,2},{4,7},{5,4},{6,5},{7,6},{8,11},{9,8},{10,9... | collective-permute-start | bytes 196616 | tf_op jit(solution)/shard_map/ppermute | solution.py:226
  91.0 5.1 %collective-permute-start.5 = (bf16[64,512]{1,0:T(8,128)(2,1)S(1)}, bf16[64,512]{1,0:T(8,128)(2,1)S(1)}, u32[]{:S(2)}, u32[]{:S(2)}) collective-permute-start(bf16[64,512]{1,0:T(8,128)(2,1)S(1)} %copy-done.7), channel_id=1, source_target_pairs={{0,2},{1,3},{2,0},{3,1},{4,6},{5,7},{6,4},{7,5},{8,10},{9,11},{10,... | collective-permute-start | bytes 196616 | tf_op jit(solution)/shard_map/ppermute | solution.py:226
  96.1 0.0 collective-permute-done.3
  96.1 0.0 collective-permute-done.4
  96.1 5.1 %collective-permute-done.5 = bf16[64,512]{1,0:T(8,128)(2,1)S(1)} collective-permute-done((bf16[64,512]{1,0:T(8,128)(2,1)S(1)}, bf16[64,512]{1,0:T(8,128)(2,1)S(1)}, u32[]{:S(2)}, u32[]{:S(2)}) %collective-permute-start.5) | collective-permute-done | bytes 65568 | tf_op jit(solution)/shard_map/ppermute | solution.py:226
  101.2 0.7 add_convert_fusion
  101.9 0.0 all-to-all-done.3
  101.9 0.7 copy-done
  102.6 1.6 %settle.1 = (f32[64,256]{1,0:T(8,128)}, f32[64,256]{1,0:T(8,128)}, f32[64,256]{1,0:T(8,128)}) custom-call(f32[512,128]{1,0:T(8,128)} %bitcast.15), custom_call_target="tpu_custom_call" | custom-call | tf_op jit(solution)/shard_map/settle/pallas_call | solution.py:286
  (13 shorter events, 0.0 us)
Async XLA Ops:
  0.6 0.9 copy-start.6
  1.5 18.2 %copy-start.1 = (bf16[128,512]{1,0:T(8,128)(2,1)}, bf16[128,512]{1,0:T(8,128)(2,1)S(1)}, u32[]{:S(2)}) copy-start(bf16[128,512]{1,0:T(8,128)(2,1)S(1)} %constant_dynamic-update-slice_fusion.own_ref) | copy-start | bytes 393220
  1.5 13.8 %collective-permute-start.2 = (bf16[128,512]{1,0:T(8,128)(2,1)S(1)}, bf16[128,512]{1,0:T(8,128)(2,1)S(1)}, u32[]{:S(2)}, u32[]{:S(2)}) collective-permute-start(bf16[128,512]{1,0:T(8,128)(2,1)S(1)} %constant_dynamic-update-slice_fusion.own_ref), channel_id=1, source_target_pairs={{0,2},{1,3},{2,0},{3,1},{4,6},{5,7},{6,4},{7,5},{8,10},{9,11},{10,... | collective-permute-start | bytes 393224 | tf_op jit(solution)/shard_map/ppermute | solution.py:226
  7.9 11.3 %collective-permute-start.1 = (bf16[128,512]{1,0:T(8,128)(2,1)S(1)}, bf16[128,512]{1,0:T(8,128)(2,1)S(1)}, u32[]{:S(2)}, u32[]{:S(2)}) collective-permute-start(bf16[128,512]{1,0:T(8,128)(2,1)S(1)} %constant_dynamic-update-slice_fusion.own_ref), channel_id=1, source_target_pairs={{0,3},{1,0},{2,1},{3,2},{4,7},{5,4},{6,5},{7,6},{8,11},{9,8},{10,9... | collective-permute-start | bytes 393224 | tf_op jit(solution)/shard_map/ppermute | solution.py:226
  8.5 11.3 %collective-permute-start = (bf16[128,512]{1,0:T(8,128)(2,1)S(1)}, bf16[128,512]{1,0:T(8,128)(2,1)S(1)}, u32[]{:S(2)}, u32[]{:S(2)}) collective-permute-start(bf16[128,512]{1,0:T(8,128)(2,1)S(1)} %constant_dynamic-update-slice_fusion.own_ref), channel_id=1, source_target_pairs={{0,1},{1,2},{2,3},{3,0},{4,5},{5,6},{6,7},{7,4},{8,9},{9,10},{10,1... | collective-permute-start | bytes 393224 | tf_op jit(solution)/shard_map/ppermute | solution.py:226
  15.3 4.5 %copy-start.3 = (bf16[128,512]{1,0:T(8,128)(2,1)}, bf16[128,512]{1,0:T(8,128)(2,1)S(1)}, u32[]{:S(2)}) copy-start(bf16[128,512]{1,0:T(8,128)(2,1)S(1)} %collective-permute-done.2.got2_ref) | copy-start | bytes 393220
  19.2 0.6 copy-start.4
  19.8 0.6 copy-start.5
  81.4 5.4 %copy-start.9 = (bf16[64,512]{1,0:T(8,128)(2,1)S(1)}, bf16[64,512]{1,0:T(8,128)(2,1)}, u32[]{:S(2)}) copy-start(bf16[64,512]{1,0:T(8,128)(2,1)} %get-tuple-element.25) | copy-start | bytes 196612
  81.4 7.7 %copy-start.8 = (bf16[64,512]{1,0:T(8,128)(2,1)S(1)}, bf16[64,512]{1,0:T(8,128)(2,1)}, u32[]{:S(2)}) copy-start(bf16[64,512]{1,0:T(8,128)(2,1)} %get-tuple-element.26) | copy-start | bytes 196612
  81.4 9.7 %copy-start.7 = (bf16[64,512]{1,0:T(8,128)(2,1)S(1)}, bf16[64,512]{1,0:T(8,128)(2,1)}, u32[]{:S(2)}) copy-start(bf16[64,512]{1,0:T(8,128)(2,1)} %get-tuple-element.27) | copy-start | bytes 196612
  81.4 19.9 %copy-start.2 = (f32[64,512]{1,0:T(8,128)S(1)}, f32[64,512]{1,0:T(8,128)}, u32[]{:S(2)}) copy-start(f32[64,512]{1,0:T(8,128)} %get-tuple-element.24) | copy-start | bytes 393220
  81.4 20.5 %all-to-all-start.3 = ((f32[64,8,128]{2,1,0:T(8,128)}), f32[64,8,128]{2,1,0:T(8,128)S(1)}, u32[]{:S(2)}, u32[]{:S(2)}) async-start(f32[64,8,128]{2,1,0:T(8,128)} %bitcast.16), calls=%async_computation.3 | async-start | bytes 524288 | tf_op jit(solution)/shard_map/all_to_all | solution.py:222
  86.8 9.3 %collective-permute-start.3 = (bf16[64,512]{1,0:T(8,128)(2,1)S(1)}, bf16[64,512]{1,0:T(8,128)(2,1)S(1)}, u32[]{:S(2)}, u32[]{:S(2)}) collective-permute-start(bf16[64,512]{1,0:T(8,128)(2,1)S(1)} %copy-done.9), channel_id=1, source_target_pairs={{0,1},{1,2},{2,3},{3,0},{4,5},{5,6},{6,7},{7,4},{8,9},{9,10},{10,1... | collective-permute-start | bytes 196616 | tf_op jit(solution)/shard_map/ppermute | solution.py:226
  89.0 7.1 %collective-permute-start.4 = (bf16[64,512]{1,0:T(8,128)(2,1)S(1)}, bf16[64,512]{1,0:T(8,128)(2,1)S(1)}, u32[]{:S(2)}, u32[]{:S(2)}) collective-permute-start(bf16[64,512]{1,0:T(8,128)(2,1)S(1)} %copy-done.8), channel_id=1, source_target_pairs={{0,3},{1,0},{2,1},{3,2},{4,7},{5,4},{6,5},{7,6},{8,11},{9,8},{10,9... | collective-permute-start | bytes 196616 | tf_op jit(solution)/shard_map/ppermute | solution.py:226
  91.0 10.2 %collective-permute-start.5 = (bf16[64,512]{1,0:T(8,128)(2,1)S(1)}, bf16[64,512]{1,0:T(8,128)(2,1)S(1)}, u32[]{:S(2)}, u32[]{:S(2)}) collective-permute-start(bf16[64,512]{1,0:T(8,128)(2,1)S(1)} %copy-done.7), channel_id=1, source_target_pairs={{0,2},{1,3},{2,0},{3,1},{4,6},{5,7},{6,4},{7,5},{8,10},{9,11},{10,... | collective-permute-start | bytes 196616 | tf_op jit(solution)/shard_map/ppermute | solution.py:226
  101.9 0.7 copy-start
where the time goes:
time: 105 us; the launch traced here: 104 us
  blocking collectives  48.5 us (46%)
  starting transfers between devices  24 us (23%)
  Pallas kernels  14.1 us (13%)
  waiting for transfers between devices  14 us (13%)
  local copies, waits for them, and re-layouts  2.25 us (2%)
    all_to_all x3, blocking collectives, exchanged(): return lax.all_to_all(parts, axis, 0, 0, tiled=True).reshape(rows.shape)  48.5 us
    ppermute x6, starting transfers between devices, shifted(): return lax.ppermute(value, 'ch', [(i, (i + shift) % 4) for i in range(4)])  18.6 us
    ppermute x6, waiting for transfers between devices, shifted(): return lax.ppermute(value, 'ch', [(i, (i + shift) % 4) for i in range(4)])  14 us
    pallas_call x1, Pallas kernels, on_device(): pl.pallas_call(convolve_kernel, out_shape=shaped((1024, LANES), BF16), in...  5.57 us
    all_to_all x1, starting transfers between devices, exchanged(): return lax.all_to_all(parts, axis, 0, 0, tiled=True).reshape(rows.shape)  5.42 us
    pallas_call x1, Pallas kernels, on_device(): pl.pallas_call(lambda *refs: gradient_kernel(*refs, scale=scale), out_sha...  2.7 us
    pallas_call x1, Pallas kernels, on_device(): pl.pallas_call(project_kernel, out_shape=(shaped((1024, LANES), BF16), sh...  2.51 us
    unnamed x21, local copies, waits for them, and re-layouts  2.25 us
  transfers between devices with their start and end apart: 7, of which 4 were waited for; matrix products, arithmetic and copies ran while one was open for 1% of the time, Pallas kernels for 0%

commit v1 on v0

v1 whole, which is shorter than its diff:
```python
import math

import jax
import jax.numpy as jnp
import ml_dtypes
import numpy as np
from jax import lax
from jax.experimental import pallas as pl
from jax.experimental.pallas import tpu as pltpu
from jax.sharding import PartitionSpec as P


F32 = jnp.float32
BF16 = jnp.bfloat16
LANES = 128
GROUP = 16


def halves(table):
    high = table.astype(ml_dtypes.bfloat16)
    low = (table - high.astype(np.float64)).astype(ml_dtypes.bfloat16)
    return high, low


def transform_tables(tokens):
    rows = tokens // LANES
    length = 2 * tokens
    per_sender = rows // 64
    order = np.arange(rows).reshape(64 // GROUP, GROUP, per_sender)
    order = order.transpose(0, 2, 1).reshape(-1)
    k1 = np.arange(rows) + 0.5
    theta = 2.0 * np.pi * ((k1[:, None] * order[None, :]) % (2 * rows)) / (2 * rows)
    outer = np.concatenate([np.cos(theta), -np.sin(theta)], axis=0)
    q = np.arange(LANES)
    phi = 2.0 * np.pi * ((q[:, None] * q[None, :]) % LANES) / LANES
    c, s = np.cos(phi), np.sin(phi)
    inner = np.block([[c, -s], [s, c]])
    twist = 2.0 * np.pi * k1[:, None] * q[None, :] / length
    twiddle = np.stack([np.cos(twist), -np.sin(twist)]).astype(np.float32)
    scale = 2.0 / length
    return (
        np.concatenate(halves(outer), axis=0),
        np.concatenate(halves(inner) + halves(inner.T), axis=0),
        np.concatenate(halves(outer.T * scale), axis=0),
        twiddle,
    )


def exchange_table(rows):
    table = np.zeros((GROUP, rows, rows, GROUP), np.float32)
    for e in range(GROUP):
        for r in range(rows):
            table[e, r, r, e] = 1.0
    return table.reshape(GROUP * rows, rows * GROUP).astype(ml_dtypes.bfloat16)


def dot(left, right, dims=((1,), (0,))):
    return lax.dot_general(left, right, (dims, ((), ())), preferred_element_type=F32)


def split_up(value):
    high = value.astype(BF16)
    return high, (value - high.astype(F32)).astype(BF16)


def dot3_left(table_high, table_low, value):
    high, low = split_up(value)
    return dot(table_high, high) + (dot(table_high, low) + dot(table_low, high))


def dot3_right(value, table_high, table_low):
    high, low = split_up(value)
    return dot(high, table_high) + (dot(low, table_high) + dot(high, table_low))


def write_messages(out_ref, swap, blocks):
    size = swap.shape[0]
    for g, block in enumerate(blocks):
        rows = jnp.concatenate(block, axis=0)
        out_ref[g * size : (g + 1) * size, :] = dot(swap, rows).astype(BF16)


def read_messages(in_ref, swap):
    size = swap.shape[0]
    return [
        dot(swap, in_ref[g * size : (g + 1) * size, :], ((0,), (0,))).astype(BF16)
        for g in range(64 // GROUP)
    ]


def lane_blocks(value):
    return [value[:, u * LANES : (u + 1) * LANES] for u in range(value.shape[1] // LANES)]


def by_run(values):
    parts = [x for value in values for x in lane_blocks(value)]
    return [[x[g * GROUP : (g + 1) * GROUP] for x in parts] for g in range(64 // GROUP)]


def whole_signal(groups, k):
    return jnp.concatenate([x[k * 64 : (k + 1) * 64] for x in groups], axis=0)


def pack_kernel(in_ref, grad_ref, *refs):
    *sources, own_ref, first, second, third, fourth, fifth, sem = refs
    pairs = [(in_ref, own_ref.at[pl.ds(0, 64), :]), (grad_ref, own_ref.at[pl.ds(64, 64), :])]
    pairs += zip(sources, (first, second, third, fourth, fifth))
    copies = [pltpu.make_async_copy(a, b, sem) for a, b in pairs]
    for copy in copies:
        copy.start()
    for copy in copies:
        copy.wait()


def project_kernel(
    ch_ref, own_ref, got1_ref, got3_ref, got2_ref, wv_ref, wg_ref, wo_ref, taps_ref, swap_ref,
    msg_ref, gate_ref, dgated_ref, in_ref, grad_ref,
):
    ch = ch_ref[0]
    for shift, ref in ((0, own_ref), (1, got1_ref), (3, got3_ref), (2, got2_ref)):
        at = pl.multiple_of(lax.rem(ch + (4 - shift), 4) * 64, 64)
        in_ref[pl.ds(at, 64), :] = ref[:64, :]
        grad_ref[pl.ds(at, 64), :] = ref[64:, :]
    full_in = in_ref[...]
    value = dot(wv_ref[...], full_in).astype(BF16)
    gate = dot(wg_ref[...], full_in)
    d_gated = dot(wo_ref[...], grad_ref[...])
    gate_ref[...] = gate
    dgated_ref[...] = d_gated
    d_mixed = (d_gated * gate).astype(BF16)
    signals = (value, d_mixed, *split_up(taps_ref[...]))
    write_messages(msg_ref, swap_ref[...], by_run(signals))


def spectrum(first, tw_re, tw_im, table_high, table_low):
    half = first.shape[0] // 2
    re, im = first[:half], first[half:]
    z = jnp.concatenate([re * tw_re - im * tw_im, re * tw_im + im * tw_re], axis=1)
    return dot3_right(z, table_high, table_low)


def convolve_kernel(got_ref, swap_ref, outer_ref, inner_ref, last_ref, tw_ref, out_ref):
    rows = outer_ref.shape[0] // 2
    size = 2 * LANES
    ih, il, jh, jl = (inner_ref[k * size : (k + 1) * size, :] for k in range(4))
    groups = read_messages(got_ref, swap_ref[...])
    v, d, high, low = (whole_signal(groups, k) for k in range(4))
    first = dot(outer_ref[:rows, :], jnp.concatenate([v, d, high, low], axis=1))
    more = dot(outer_ref[rows:, :], jnp.concatenate([v, d, high], axis=1))
    tw_re, tw_im = tw_ref[0], tw_ref[1]
    firsts, mores = lane_blocks(first), lane_blocks(more)
    firsts = [firsts[0] + mores[0], firsts[1] + mores[1], firsts[2] + firsts[3] + mores[2]]
    v, d, h = (lane_blocks(spectrum(x, tw_re, tw_im, ih, il)) for x in firsts)
    (v_re, v_im), (d_re, d_im), (h_re, h_im) = v, d, h
    products = (
        (h_re * v_re - h_im * v_im, h_re * v_im + h_im * v_re),
        (h_re * d_re + h_im * d_im, h_re * d_im - h_im * d_re),
        (v_re * d_re + v_im * d_im, v_re * d_im - v_im * d_re),
    )
    back = []
    for re, im in products:
        y = dot3_right(jnp.concatenate([re, im], axis=1), jh, jl)
        re, im = lane_blocks(y)
        b = jnp.concatenate([re * tw_re + im * tw_im, im * tw_re - re * tw_im], axis=0)
        back.append(dot3_left(last_ref[: rows // 2, :], last_ref[rows // 2 :, :], b))
    mixed, d_value, d_filter = back
    signals = (mixed.astype(BF16), d_value.astype(BF16), *split_up(d_filter))
    blocks = [[x[g * 64 : (g + 1) * 64] for x in signals] for g in range(64 // GROUP)]
    write_messages(out_ref, swap_ref[...], blocks)


def gradient_kernel(
    ch_ref, got_ref, swap_ref, gate_ref, dgated_ref, in_ref, grad_ref, wv_ref, wg_ref,
    sums_ref, own_ref, send1_ref, send3_ref, send2_ref, filt_ref, part_ref, *, scale
):
    groups = read_messages(got_ref, swap_ref[...])

    def signal(k):
        cols = []
        for u in range(4):
            at = (k * 4 + u) * GROUP
            cols.append(jnp.concatenate([x[at : at + GROUP] for x in groups], axis=0))
        return jnp.concatenate(cols, axis=1)

    mixed = signal(0).astype(F32)
    d_value = signal(1)
    filt_ref[...] = (signal(2).astype(F32) + signal(3).astype(F32)) * scale
    gated_out = (gate_ref[...] * mixed).astype(BF16)
    d_gate = (dgated_ref[...] * mixed).astype(BF16)
    both = jnp.concatenate([d_value, d_gate], axis=0)
    weights = jnp.concatenate([wv_ref[...], wg_ref[...]], axis=0)
    part_ref[...] = dot(weights, both, ((0,), (0,)))
    ch = ch_ref[0]

    def block(shift):
        at = pl.multiple_of(lax.rem(ch + shift, 4) * 64, 64)
        return part_ref[pl.ds(at, 64), :]

    own_ref[...] = block(0)
    send1_ref[...] = block(1).astype(BF16)
    send3_ref[...] = block(3).astype(BF16)
    send2_ref[...] = block(2).astype(BF16)
    term = dot(both, in_ref[...], ((1,), (1,)))
    out_term = dot(gated_out, grad_ref[...], ((1,), (1,)))
    tiles = []
    for value in (term, out_term):
        for a in range(value.shape[0] // 8):
            tiles += lane_blocks(value[8 * a : 8 * a + 8])
    tiles += [jnp.zeros_like(tiles[0])] * (64 - len(tiles))
    sums_ref[...] = jnp.concatenate(tiles, axis=0).astype(BF16)


def total_kernel(got_ref, out_ref, *, scale):
    total = got_ref[...].astype(F32).reshape(64, 8, LANES).sum(axis=0) * scale
    whole = jnp.broadcast_to(total[None], (64, 8, LANES)).reshape(512, LANES)
    out_ref[...] = whole.astype(BF16)


def settle_kernel(
    got_ref, own_ref, came1_ref, came3_ref, came2_ref, din_ref, dwv_ref, dwg_ref, dwo_ref
):
    d_inputs = own_ref[...]
    for ref in (came1_ref, came3_ref, came2_ref):
        d_inputs = d_inputs + ref[...].astype(F32)
    din_ref[...] = d_inputs.astype(BF16)
    for k, ref in enumerate((dwv_ref, dwg_ref, dwo_ref)):
        for a in range(8):
            at = 16 * (8 * k + a)
            pair = got_ref[at : at + 16, :].astype(F32)
            ref[8 * a : 8 * a + 8, :] = jnp.concatenate([pair[:8], pair[8:]], axis=1)


ANY = pl.BlockSpec(memory_space=pl.ANY)
VMEM = pl.BlockSpec(memory_space=pltpu.VMEM)
SMEM = pl.BlockSpec(memory_space=pltpu.SMEM)


def near(value):
    return pltpu.with_memory_space_constraint(value, pltpu.VMEM)


def far(value):
    return pltpu.with_memory_space_constraint(value, pltpu.HBM)


def call(kernel, outs, *args, scalar=None, scratch=()):
    many = isinstance(outs, list)
    specs = [VMEM] * len(args)
    args = [near(x) for x in args]
    if scalar is not None:
        specs, args = ([SMEM] + specs, [scalar] + args)
    return pl.pallas_call(
        kernel,
        out_shape=tuple(outs) if many else outs,
        in_specs=specs,
        out_specs=(VMEM,) * len(outs) if many else VMEM,
        scratch_shapes=scratch,
        compiler_params=pltpu.CompilerParams(vmem_limit_bytes=16 << 20),
    )(*args)


def packed(inputs, grad_out, *rest):
    outs = [pltpu.VMEM((2 * inputs.shape[0], inputs.shape[1]), inputs.dtype)]
    outs += [pltpu.VMEM(x.shape, x.dtype) for x in rest]
    return pl.pallas_call(
        pack_kernel,
        out_shape=tuple(outs),
        in_specs=[ANY] * (2 + len(rest)),
        out_specs=(VMEM,) * len(outs),
        scratch_shapes=[pltpu.SemaphoreType.DMA(())],
        compiler_params=pltpu.CompilerParams(vmem_limit_bytes=16 << 20),
        name="pack",
    )(*[far(x) for x in (inputs, grad_out, *rest)])


def exchanged(rows, axis):
    count = lax.axis_size(axis)
    parts = rows.reshape(count, rows.shape[0] // count, rows.shape[1])
    return lax.all_to_all(parts, axis, 0, 0, tiled=True).reshape(rows.shape)


def shifted(value, shift):
    return lax.ppermute(value, "ch", [(i, (i + shift) % 4) for i in range(4)])


def on_device(inputs, w_value, w_gate, w_out, filter_taps, grad_out):
    tokens = filter_taps.shape[1] * lax.axis_size("seq")
    scale = 1.0 / math.sqrt(tokens)
    outer, inner, last, twiddle = [jnp.asarray(t) for t in transform_tables(tokens)]
    swap = jnp.asarray(exchange_table(16))
    ch = lax.axis_index("ch").astype(jnp.int32).reshape(1)
    inside = pltpu.VMEM
    outside = jax.ShapeDtypeStruct

    own, wv, wg, wo, taps, tw = packed(
        inputs, grad_out, w_value.T, w_gate.T, w_out, filter_taps, twiddle
    )
    got = [shifted(own, s) for s in (1, 3, 2)]
    msg, gate, d_gated, full_in, full_grad = call(
        project_kernel,
        [
            inside((1024, LANES), BF16),
            inside((64, 512), F32),
            inside((64, 512), F32),
            inside((256, 512), BF16),
            inside((256, 512), BF16),
        ],
        own, *got, wv, wg, wo, taps, swap, scalar=ch,
    )
    back = call(
        convolve_kernel, inside((1024, LANES), BF16),
        exchanged(msg, "seq"), swap, outer, inner, last, tw,
    )
    sums, mine, send1, send3, send2, d_filter = call(
        lambda *refs: gradient_kernel(*refs, scale=scale),
        [
            inside((512, LANES), BF16),
            inside((64, 512), F32),
            inside((64, 512), BF16),
            inside((64, 512), BF16),
            inside((64, 512), BF16),
            outside((64, 512), F32),
        ],
        exchanged(back, "seq"), swap, gate, d_gated, full_in, full_grad, wv, wg,
        scalar=ch, scratch=[pltpu.VMEM((256, 512), F32)],
    )
    arrived = exchanged(sums, "seq")
    came = [shifted(x, s) for x, s in ((send2, 2), (send3, 3), (send1, 1))]
    total = call(
        lambda *refs: total_kernel(*refs, scale=scale),
        inside((512, LANES), BF16), arrived,
    )
    d_inputs, dwv, dwg, dwo = call(
        settle_kernel,
        [outside((64, 512), BF16)] + [outside((64, 256), F32)] * 3,
        exchanged(total, "seq"), mine, *came,
    )
    return d_inputs, dwv.T, dwg.T, dwo, d_filter


def solution(mesh):
    placed = (
        P("ch", "seq"),
        P(None, "ch"),
        P(None, "ch"),
        P("ch", None),
        P("ch", "seq"),
        P("ch", "seq"),
    )
    return jax.shard_map(
        on_device,
        mesh=mesh,
        in_specs=placed,
        out_specs=(P("ch", "seq"), P(None, "ch"), P(None, "ch"), P("ch", None), P("ch", "seq")),
        check_vma=False,
    )
```

time: 105 us -> 91.8 us (0.87)
  the two profiles are of different devices: /device:TPU:32 before, /device:TPU:1 now
where the time goes in v1:
time: 91.8 us; the launch traced here: 91.5 us
  blocking collectives  44.3 us (48%)
  starting transfers between devices  21.9 us (24%)
  waiting for transfers between devices  16.9 us (18%)
  Pallas kernels  7.76 us (8%)
    all_to_all x3, blocking collectives, exchanged(): return lax.all_to_all(parts, axis, 0, 0, tiled=True).reshape(rows.shape)  44.3 us
    ppermute x6, starting transfers between devices, shifted(): return lax.ppermute(value, 'ch', [(i, (i + shift) % 4) for i in range(4)])  17.4 us
    ppermute x6, waiting for transfers between devices, shifted(): return lax.ppermute(value, 'ch', [(i, (i + shift) % 4) for i in range(4)])  16.9 us
    pallas_call x5, Pallas kernels, call(): pl.pallas_call(kernel, out_shape=tuple(outs) if many else outs, in_specs=...  6.56 us
    all_to_all x1, starting transfers between devices, exchanged(): return lax.all_to_all(parts, axis, 0, 0, tiled=True).reshape(rows.shape)  4.43 us
  transfers between devices with their start and end apart: 7, of which 4 were waited for; matrix products, arithmetic and copies ran while one was open for 0% of the time, Pallas kernels for 0%

profile of v1, /device:TPU:1, one launch (start us, length us, event | category | flops | bytes accessed | tf_op | source)
XLA Modules:
  0.0 91.5 jit_solution(4572682297784928957)
XLA Ops:
  0.6 0.0 copy-start
  0.6 0.0 copy-start.3
  0.7 1.2 %pack.1 = (bf16[128,512]{1,0:T(8,128)(2,1)S(1)}, bf16[64,256]{1,0:T(8,128)(2,1)S(1)}, bf16[64,256]{1,0:T(8,128)(2,1)S(1)}, bf16[64,256]{1,0:T(8,128)(2,1)S(1)}, ...) custom-call(bf16[64,512]{1,0:T(8,128)(2,1)} %in_ref.1, bf16[64,512]{1,0:T(8,128)(2,1)} %grad_ref.1, ...), custom_call_target="tpu_custom_call" | custom-call | tf_op jit(solution)/shard_map/pack/pallas_call | solution.py:265
  1.9 7.8 %collective-permute-start.2 = (bf16[128,512]{1,0:T(8,128)(2,1)S(1)}, bf16[128,512]{1,0:T(8,128)(2,1)S(1)}, u32[]{:S(2)}, u32[]{:S(2)}) collective-permute-start(bf16[128,512]{1,0:T(8,128)(2,1)S(1)} %get-tuple-element.26.own_ref), channel_id=1, source_target_pairs={{0,2},{1,3},{2,0},{3,1},{4,6},{5,7},{6,4},{7,5},{8,10},{9,11},{10,... | collective-permute-start | bytes 393224 | tf_op jit(solution)/shard_map/ppermute | solution.py:283
  9.7 0.0 collective-permute-start.1
  9.7 2.4 %collective-permute-start = (bf16[128,512]{1,0:T(8,128)(2,1)S(1)}, bf16[128,512]{1,0:T(8,128)(2,1)S(1)}, u32[]{:S(2)}, u32[]{:S(2)}) collective-permute-start(bf16[128,512]{1,0:T(8,128)(2,1)S(1)} %get-tuple-element.26.own_ref), channel_id=1, source_target_pairs={{0,1},{1,2},{2,3},{3,0},{4,5},{5,6},{6,7},{7,4},{8,9},{9,10},{10,1... | collective-permute-start | bytes 393224 | tf_op jit(solution)/shard_map/ppermute | solution.py:283
  12.0 0.4 collective-permute-done.2.got2_ref
  12.4 10.1 %collective-permute-done.1.got3_ref = bf16[128,512]{1,0:T(8,128)(2,1)S(1)} collective-permute-done((bf16[128,512]{1,0:T(8,128)(2,1)S(1)}, bf16[128,512]{1,0:T(8,128)(2,1)S(1)}, u32[]{:S(2)}, u32[]{:S(2)}) %collective-permute-start.1) | collective-permute-done | bytes 131104 | tf_op jit(solution)/shard_map/ppermute | solution.py:283
  22.6 0.0 collective-permute-done.got1_ref
  22.6 0.0 copy-done
  22.6 0.0 copy-start.1
  22.6 0.0 copy-start.2
  22.6 0.6 shard_map.146
  23.2 17.5 %all_to_all.20 = bf16[64,16,128]{2,1,0:T(8,128)(2,1)S(1)} all-to-all(bf16[64,16,128]{2,1,0:T(8,128)(2,1)S(1)} %bitcast.18), channel_id=1, replica_groups=mesh['seq'=64,'ch'=4] {'seq'}, dimensions={0} | all-to-all | bytes 524288 | tf_op jit(solution)/shard_map/all_to_all | solution.py:279
  40.7 0.0 copy-done.3
  40.7 0.0 copy-done.1
  40.7 0.0 copy-done.2
  40.7 3.3 %shard_map.147 = bf16[1024,128]{1,0:T(8,128)(2,1)S(1)} custom-call(bf16[1024,128]{1,0:T(8,128)(2,1)S(1)} %bitcast.13, bf16[256,256]{1,0:T(8,128)(2,1)S(1)} %copy-done, bf16[1024,256]{1,0:T(8,128)(2,1)S(1)} %copy-done.3, bf16[1024,256]{1,0:T(8,128)(2,1)S(1)} %copy-done.2, bf16[512,512]{1,0:T(8,128)(2,1)S(1)} %copy-done.1, ...), custom_call_target="tpu_custom_call" | custom-call | tf_op jit(solution)/shard_map/pallas_call | solution.py:252
  44.0 14.0 %all_to_all.21 = bf16[64,16,128]{2,1,0:T(8,128)(2,1)S(1)} all-to-all(bf16[64,16,128]{2,1,0:T(8,128)(2,1)S(1)} %bitcast.14), channel_id=1, replica_groups=mesh['seq'=64,'ch'=4] {'seq'}, dimensions={0} | all-to-all | bytes 524288 | tf_op jit(solution)/shard_map/all_to_all | solution.py:279
  58.0 1.3 %shard_map.148 = (bf16[512,128]{1,0:T(8,128)(2,1)S(1)}, f32[64,512]{1,0:T(8,128)S(1)}, bf16[64,512]{1,0:T(8,128)(2,1)S(1)}, bf16[64,512]{1,0:T(8,128)(2,1)S(1)},...) custom-call(s32[1]{0:T(128)} %bitcast.ch_ref.refs_0_, bf16[1024,128]{1,0:T(8,128)(2,1)S(1)} %bitcast.15, ...), custom_call_target="tpu_custom_call" | custom-call | tf_op jit(solution)/shard_map/pallas_call | solution.py:252
  59.2 12.7 %all_to_all.22 = bf16[64,8,128]{2,1,0:T(8,128)(2,1)S(1)} all-to-all(bf16[64,8,128]{2,1,0:T(8,128)(2,1)S(1)} %bitcast.19), channel_id=1, replica_groups=mesh['seq'=64,'ch'=4] {'seq'}, dimensions={0} | all-to-all | bytes 262144 | tf_op jit(solution)/shard_map/all_to_all | solution.py:279
  72.0 0.7 shard_map.149
  72.7 4.4 %all-to-all-start.3 = ((bf16[64,8,128]{2,1,0:T(8,128)(2,1)}), bf16[64,8,128]{2,1,0:T(8,128)(2,1)S(1)}, u32[]{:S(2)}, u32[]{:S(2)}) async-start(bf16[64,8,128]{2,1,0:T(8,128)(2,1)} %bitcast.9), calls=%async_computation.3 | async-start | bytes 262144 | tf_op jit(solution)/shard_map/all_to_all | solution.py:279
  77.2 4.9 %collective-permute-start.3 = (bf16[64,512]{1,0:T(8,128)(2,1)S(1)}, bf16[64,512]{1,0:T(8,128)(2,1)S(1)}, u32[]{:S(2)}, u32[]{:S(2)}) collective-permute-start(bf16[64,512]{1,0:T(8,128)(2,1)S(1)} %get-tuple-element.39), channel_id=1, source_target_pairs={{0,2},{1,3},{2,0},{3,1},{4,6},{5,7},{6,4},{7,5},{8,10},{9,11},{10,... | collective-permute-start | bytes 196616 | tf_op jit(solution)/shard_map/ppermute | solution.py:283
  82.1 0.4 collective-permute-start.4
  82.4 2.0 %collective-permute-start.5 = (bf16[64,512]{1,0:T(8,128)(2,1)S(1)}, bf16[64,512]{1,0:T(8,128)(2,1)S(1)}, u32[]{:S(2)}, u32[]{:S(2)}) collective-permute-start(bf16[64,512]{1,0:T(8,128)(2,1)S(1)} %get-tuple-element.41), channel_id=1, source_target_pairs={{0,1},{1,2},{2,3},{3,0},{4,5},{5,6},{6,7},{7,4},{8,9},{9,10},{10,1... | collective-permute-start | bytes 196616 | tf_op jit(solution)/shard_map/ppermute | solution.py:283
  84.4 0.8 collective-permute-done.3.came1_ref
  85.3 5.5 %collective-permute-done.4.came3_ref = bf16[64,512]{1,0:T(8,128)(2,1)S(1)} collective-permute-done((bf16[64,512]{1,0:T(8,128)(2,1)S(1)}, bf16[64,512]{1,0:T(8,128)(2,1)S(1)}, u32[]{:S(2)}, u32[]{:S(2)}) %collective-permute-start.4) | collective-permute-done | bytes 65568 | tf_op jit(solution)/shard_map/ppermute | solution.py:283
  90.8 0.0 collective-permute-done.5.came2_ref
  90.8 0.0 all-to-all-done.3
  90.8 0.7 shard_map.150
Async XLA Ops:
  0.6 21.9 %copy-start = (bf16[256,256]{1,0:T(8,128)(2,1)S(1)}, bf16[256,256]{1,0:T(8,128)(2,1)}, u32[]{:S(2)}) copy-start(bf16[256,256]{1,0:T(8,128)(2,1)} %constant.18.clone.swap_ref.refs_2_) | copy-start | bytes 393220
  0.6 40.0 %copy-start.3 = (bf16[1024,256]{1,0:T(8,128)(2,1)S(1)}, bf16[1024,256]{1,0:T(8,128)(2,1)}, u32[]{:S(2)}) copy-start(bf16[1024,256]{1,0:T(8,128)(2,1)} %constant.14.clone.outer_ref) | copy-start | bytes 1572868
  1.9 10.6 %collective-permute-start.2 = (bf16[128,512]{1,0:T(8,128)(2,1)S(1)}, bf16[128,512]{1,0:T(8,128)(2,1)S(1)}, u32[]{:S(2)}, u32[]{:S(2)}) collective-permute-start(bf16[128,512]{1,0:T(8,128)(2,1)S(1)} %get-tuple-element.26.own_ref), channel_id=1, source_target_pairs={{0,2},{1,3},{2,0},{3,1},{4,6},{5,7},{6,4},{7,5},{8,10},{9,11},{10,... | collective-permute-start | bytes 393224 | tf_op jit(solution)/shard_map/ppermute | solution.py:283
  9.7 12.9 %collective-permute-start.1 = (bf16[128,512]{1,0:T(8,128)(2,1)S(1)}, bf16[128,512]{1,0:T(8,128)(2,1)S(1)}, u32[]{:S(2)}, u32[]{:S(2)}) collective-permute-start(bf16[128,512]{1,0:T(8,128)(2,1)S(1)} %get-tuple-element.26.own_ref), channel_id=1, source_target_pairs={{0,3},{1,0},{2,1},{3,2},{4,7},{5,4},{6,5},{7,6},{8,11},{9,8},{10,9... | collective-permute-start | bytes 393224 | tf_op jit(solution)/shard_map/ppermute | solution.py:283
  9.7 12.9 %collective-permute-start = (bf16[128,512]{1,0:T(8,128)(2,1)S(1)}, bf16[128,512]{1,0:T(8,128)(2,1)S(1)}, u32[]{:S(2)}, u32[]{:S(2)}) collective-permute-start(bf16[128,512]{1,0:T(8,128)(2,1)S(1)} %get-tuple-element.26.own_ref), channel_id=1, source_target_pairs={{0,1},{1,2},{2,3},{3,0},{4,5},{5,6},{6,7},{7,4},{8,9},{9,10},{10,1... | collective-permute-start | bytes 393224 | tf_op jit(solution)/shard_map/ppermute | solution.py:283
  22.6 18.1 %copy-start.1 = (bf16[512,512]{1,0:T(8,128)(2,1)S(1)}, bf16[512,512]{1,0:T(8,128)(2,1)}, u32[]{:S(2)}) copy-start(bf16[512,512]{1,0:T(8,128)(2,1)} %constant.16.clone.last_ref) | copy-start | bytes 1572868
  22.6 18.1 %copy-start.2 = (bf16[1024,256]{1,0:T(8,128)(2,1)S(1)}, bf16[1024,256]{1,0:T(8,128)(2,1)}, u32[]{:S(2)}) copy-start(bf16[1024,256]{1,0:T(8,128)(2,1)} %constant.15.clone.inner_ref) | copy-start | bytes 1572868
  72.7 18.1 %all-to-all-start.3 = ((bf16[64,8,128]{2,1,0:T(8,128)(2,1)}), bf16[64,8,128]{2,1,0:T(8,128)(2,1)S(1)}, u32[]{:S(2)}, u32[]{:S(2)}) async-start(bf16[64,8,128]{2,1,0:T(8,128)(2,1)} %bitcast.9), calls=%async_computation.3 | async-start | bytes 262144 | tf_op jit(solution)/shard_map/all_to_all | solution.py:279
  77.2 8.1 %collective-permute-start.3 = (bf16[64,512]{1,0:T(8,128)(2,1)S(1)}, bf16[64,512]{1,0:T(8,128)(2,1)S(1)}, u32[]{:S(2)}, u32[]{:S(2)}) collective-permute-start(bf16[64,512]{1,0:T(8,128)(2,1)S(1)} %get-tuple-element.39), channel_id=1, source_target_pairs={{0,2},{1,3},{2,0},{3,1},{4,6},{5,7},{6,4},{7,5},{8,10},{9,11},{10,... | collective-permute-start | bytes 196616 | tf_op jit(solution)/shard_map/ppermute | solution.py:283
  82.1 8.7 %collective-permute-start.4 = (bf16[64,512]{1,0:T(8,128)(2,1)S(1)}, bf16[64,512]{1,0:T(8,128)(2,1)S(1)}, u32[]{:S(2)}, u32[]{:S(2)}) collective-permute-start(bf16[64,512]{1,0:T(8,128)(2,1)S(1)} %get-tuple-element.40), channel_id=1, source_target_pairs={{0,3},{1,0},{2,1},{3,2},{4,7},{5,4},{6,5},{7,6},{8,11},{9,8},{10,9... | collective-permute-start | bytes 196616 | tf_op jit(solution)/shard_map/ppermute | solution.py:283
  82.4 8.4 %collective-permute-start.5 = (bf16[64,512]{1,0:T(8,128)(2,1)S(1)}, bf16[64,512]{1,0:T(8,128)(2,1)S(1)}, u32[]{:S(2)}, u32[]{:S(2)}) collective-permute-start(bf16[64,512]{1,0:T(8,128)(2,1)S(1)} %get-tuple-element.41), channel_id=1, source_target_pairs={{0,1},{1,2},{2,3},{3,0},{4,5},{5,6},{6,7},{7,4},{8,9},{9,10},{10,1... | collective-permute-start | bytes 196616 | tf_op jit(solution)/shard_map/ppermute | solution.py:283

commit v2 on v1

--- a/solution.py
+++ b/solution.py
@@ -63,14 +63,14 @@
     return high, (value - high.astype(F32)).astype(BF16)
 
 
-def dot3_left(table_high, table_low, value):
-    high, low = split_up(value)
-    return dot(table_high, high) + (dot(table_high, low) + dot(table_low, high))
-
-
-def dot3_right(value, table_high, table_low):
-    high, low = split_up(value)
-    return dot(high, table_high) + (dot(low, table_high) + dot(high, table_low))
+def dot_left(table_high, table_low, value):
+    value = value.astype(BF16)
+    return dot(table_high, value) + dot(table_low, value)
+
+
+def dot_right(value, table_high, table_low):
+    value = value.astype(BF16)
+    return dot(value, table_high) + dot(value, table_low)
 
 
 def write_messages(out_ref, swap, blocks):
@@ -101,11 +101,22 @@
     return jnp.concatenate([x[k * 64 : (k + 1) * 64] for x in groups], axis=0)
 
 
-def pack_kernel(in_ref, grad_ref, *refs):
-    *sources, own_ref, first, second, third, fourth, fifth, sem = refs
-    pairs = [(in_ref, own_ref.at[pl.ds(0, 64), :]), (grad_ref, own_ref.at[pl.ds(64, 64), :])]
-    pairs += zip(sources, (first, second, third, fourth, fifth))
-    copies = [pltpu.make_async_copy(a, b, sem) for a, b in pairs]
+def pack_kernel(in_ref, grad_ref, own_ref, sem):
+    half = own_ref.shape[0] // 2
+    copies = [
+        pltpu.make_async_copy(in_ref, own_ref.at[pl.ds(0, half), :], sem),
+        pltpu.make_async_copy(grad_ref, own_ref.at[pl.ds(half, half), :], sem),
+    ]
+    for copy in copies:
+        copy.start()
+    for copy in copies:
+        copy.wait()
+
+
+def fetch_kernel(*refs):
+    *refs, sem = refs
+    count = len(refs) // 2
+    copies = [pltpu.make_async_copy(a, b, sem) for a, b in zip(refs[:count], refs[count:])]
     for copy in copies:
         copy.start()
     for copy in copies:
@@ -136,7 +147,7 @@
     half = first.shape[0] // 2
     re, im = first[:half], first[half:]
     z = jnp.concatenate([re * tw_re - im * tw_im, re * tw_im + im * tw_re], axis=1)
-    return dot3_right(z, table_high, table_low)
+    return dot_right(z, table_high, table_low)
 
 
 def convolve_kernel(got_ref, swap_ref, outer_ref, inner_ref, last_ref, tw_ref, out_ref):
@@ -159,10 +170,10 @@
     )
     back = []
     for re, im in products:
-        y = dot3_right(jnp.concatenate([re, im], axis=1), jh, jl)
+        y = dot_right(jnp.concatenate([re, im], axis=1), jh, jl)
         re, im = lane_blocks(y)
         b = jnp.concatenate([re * tw_re + im * tw_im, im * tw_re - re * tw_im], axis=0)
-        back.append(dot3_left(last_ref[: rows // 2, :], last_ref[rows // 2 :, :], b))
+        back.append(dot_left(last_ref[: rows // 2, :], last_ref[rows // 2 :, :], b))
     mixed, d_value, d_filter = back
     signals = (mixed.astype(BF16), d_value.astype(BF16), *split_up(d_filter))
     blocks = [[x[g * 64 : (g + 1) * 64] for x in signals] for g in range(64 // GROUP)]
@@ -259,18 +270,15 @@
     )(*args)
 
 
-def packed(inputs, grad_out, *rest):
-    outs = [pltpu.VMEM((2 * inputs.shape[0], inputs.shape[1]), inputs.dtype)]
-    outs += [pltpu.VMEM(x.shape, x.dtype) for x in rest]
+def copied(kernel, outs, *args):
     return pl.pallas_call(
-        pack_kernel,
+        kernel,
         out_shape=tuple(outs),
-        in_specs=[ANY] * (2 + len(rest)),
+        in_specs=[ANY] * len(args),
         out_specs=(VMEM,) * len(outs),
         scratch_shapes=[pltpu.SemaphoreType.DMA(())],
         compiler_params=pltpu.CompilerParams(vmem_limit_bytes=16 << 20),
-        name="pack",
-    )(*[far(x) for x in (inputs, grad_out, *rest)])
+    )(*[far(x) for x in args])
 
 
 def exchanged(rows, axis):
@@ -292,10 +300,11 @@
     inside = pltpu.VMEM
     outside = jax.ShapeDtypeStruct
 
-    own, wv, wg, wo, taps, tw = packed(
-        inputs, grad_out, w_value.T, w_gate.T, w_out, filter_taps, twiddle
-    )
+    rows, length = inputs.shape
+    (own,) = copied(pack_kernel, [inside((2 * rows, length), inputs.dtype)], inputs, grad_out)
+    later = (w_value.T, w_gate.T, w_out, filter_taps, twiddle)
     got = [shifted(own, s) for s in (1, 3, 2)]
+    wv, wg, wo, taps, tw = copied(fetch_kernel, [inside(x.shape, x.dtype) for x in later], *later)
     msg, gate, d_gated, full_in, full_grad = call(
         project_kernel,
         [
@@ -325,15 +334,17 @@
         scalar=ch, scratch=[pltpu.VMEM((256, 512), F32)],
     )
     arrived = exchanged(sums, "seq")
-    came = [shifted(x, s) for x, s in ((send2, 2), (send3, 3), (send1, 1))]
+    came2, came1 = shifted(send2, 2), shifted(send1, 1)
     total = call(
         lambda *refs: total_kernel(*refs, scale=scale),
         inside((512, LANES), BF16), arrived,
     )
+    spread = exchanged(total, "seq")
+    came3 = shifted(send3, 3)
     d_inputs, dwv, dwg, dwo = call(
         settle_kernel,
         [outside((64, 512), BF16)] + [outside((64, 256), F32)] * 3,
-        exchanged(total, "seq"), mine, *came,
+        spread, mine, came1, came3, came2,
     )
     return d_inputs, dwv.T, dwg.T, dwo, d_filter
 

time: 91.8 us -> 90.1 us (0.981)
  the two profiles are of different devices: /device:TPU:1 before, /device:TPU:32 now
where the time goes in v2:
time: 90.1 us; the launch traced here: 89.8 us
  blocking collectives  44.6 us (50%)
  starting transfers between devices  24 us (27%)
  waiting for transfers between devices  12.6 us (14%)
  Pallas kernels  7.86 us (9%)
    all_to_all x3, blocking collectives, exchanged(): return lax.all_to_all(parts, axis, 0, 0, tiled=True).reshape(rows.shape)  44.6 us
    ppermute x6, starting transfers between devices, shifted(): return lax.ppermute(value, 'ch', [(i, (i + shift) % 4) for i in range(4)])  18.6 us
    ppermute x6, waiting for transfers between devices, shifted(): return lax.ppermute(value, 'ch', [(i, (i + shift) % 4) for i in range(4)])  12.6 us
    pallas_call x5, Pallas kernels, call(): pl.pallas_call(kernel, out_shape=tuple(outs) if many else outs, in_specs=...  5.84 us
    all_to_all x1, starting transfers between devices, exchanged(): return lax.all_to_all(parts, axis, 0, 0, tiled=True).reshape(rows.shape)  5.42 us
    pallas_call x2, Pallas kernels, copied(): pl.pallas_call(kernel, out_shape=tuple(outs), in_specs=[ANY] * len(args),...  2.03 us
  transfers between devices with their start and end apart: 7, of which 4 were waited for; matrix products, arithmetic and copies ran while one was open for 0% of the time, Pallas kernels for 1%

profile of v2, /device:TPU:32, one launch (start us, length us, event | category | flops | bytes accessed | tf_op | source)
XLA Modules:
  0.0 89.8 jit_solution(12961023737667114916)
XLA Ops:
  0.6 0.9 shard_map.146.own_ref
  1.5 6.4 %collective-permute-start.2 = (bf16[128,512]{1,0:T(8,128)(2,1)S(1)}, bf16[128,512]{1,0:T(8,128)(2,1)S(1)}, u32[]{:S(2)}, u32[]{:S(2)}) collective-permute-start(bf16[128,512]{1,0:T(8,128)(2,1)S(1)} %shard_map.146.own_ref), channel_id=1, source_target_pairs={{0,2},{1,3},{2,0},{3,1},{4,6},{5,7},{6,4},{7,5},{8,10},{9,11},{10,... | collective-permute-start | bytes 393224 | tf_op jit(solution)/shard_map/ppermute | solution.py:291
  7.9 0.6 collective-permute-start.1
  8.4 2.4 %collective-permute-start = (bf16[128,512]{1,0:T(8,128)(2,1)S(1)}, bf16[128,512]{1,0:T(8,128)(2,1)S(1)}, u32[]{:S(2)}, u32[]{:S(2)}) collective-permute-start(bf16[128,512]{1,0:T(8,128)(2,1)S(1)} %shard_map.146.own_ref), channel_id=1, source_target_pairs={{0,1},{1,2},{2,3},{3,0},{4,5},{5,6},{6,7},{7,4},{8,9},{9,10},{10,1... | collective-permute-start | bytes 393224 | tf_op jit(solution)/shard_map/ppermute | solution.py:291
  10.8 0.0 copy-start
  10.8 0.0 copy-start.3
  10.8 1.1 %shard_map.147 = (bf16[64,256]{1,0:T(8,128)(2,1)S(1)}, bf16[64,256]{1,0:T(8,128)(2,1)S(1)}, bf16[64,256]{1,0:T(8,128)(2,1)S(1)}, f32[64,512]{1,0:T(8,128)S(1)}, f32[2,256,128]{2,1,0:T(8,128)S(1)}) custom-call(bf16[64,256]{1,0:T(8,128)(2,1)} %bitcast.20, bf16[64,256]{1,0:T(8,128)(2,1)} %bitcast.21, bf16[64,256]{1,0:T(8,128)(2,1)} %refs_2_.2, ...), custom_call_target="tpu_custom_call" | custom-call | tf_op jit(solution)/shard_map/pallas_call | solution.py:274
  12.0 3.3 %collective-permute-done.2.got2_ref = bf16[128,512]{1,0:T(8,128)(2,1)S(1)} collective-permute-done((bf16[128,512]{1,0:T(8,128)(2,1)S(1)}, bf16[128,512]{1,0:T(8,128)(2,1)S(1)}, u32[]{:S(2)}, u32[]{:S(2)}) %collective-permute-start.2) | collective-permute-done | bytes 131104 | tf_op jit(solution)/shard_map/ppermute | solution.py:291
  15.3 3.9 %collective-permute-done.1.got3_ref = bf16[128,512]{1,0:T(8,128)(2,1)S(1)} collective-permute-done((bf16[128,512]{1,0:T(8,128)(2,1)S(1)}, bf16[128,512]{1,0:T(8,128)(2,1)S(1)}, u32[]{:S(2)}, u32[]{:S(2)}) %collective-permute-start.1) | collective-permute-done | bytes 131104 | tf_op jit(solution)/shard_map/ppermute | solution.py:291
  19.2 0.6 collective-permute-done.got1_ref
  19.7 0.0 copy-done
  19.7 0.0 copy-start.1
  19.7 0.0 copy-start.2
  19.7 0.5 shard_map.148
  20.3 18.1 %all_to_all.20 = bf16[64,16,128]{2,1,0:T(8,128)(2,1)S(1)} all-to-all(bf16[64,16,128]{2,1,0:T(8,128)(2,1)S(1)} %bitcast.18), channel_id=1, replica_groups=mesh['seq'=64,'ch'=4] {'seq'}, dimensions={0} | all-to-all | bytes 524288 | tf_op jit(solution)/shard_map/all_to_all | solution.py:287
  38.4 0.0 copy-done.3
  38.4 0.0 copy-done.1
  38.4 0.0 copy-done.2
  38.4 2.6 %shard_map.149 = bf16[1024,128]{1,0:T(8,128)(2,1)S(1)} custom-call(bf16[1024,128]{1,0:T(8,128)(2,1)S(1)} %bitcast.13, bf16[256,256]{1,0:T(8,128)(2,1)S(1)} %copy-done, bf16[1024,256]{1,0:T(8,128)(2,1)S(1)} %copy-done.3, bf16[1024,256]{1,0:T(8,128)(2,1)S(1)} %copy-done.2, bf16[512,512]{1,0:T(8,128)(2,1)S(1)} %copy-done.1, ...), custom_call_target="tpu_custom_call" | custom-call | tf_op jit(solution)/shard_map/pallas_call | solution.py:263
  40.9 14.0 %all_to_all.21 = bf16[64,16,128]{2,1,0:T(8,128)(2,1)S(1)} all-to-all(bf16[64,16,128]{2,1,0:T(8,128)(2,1)S(1)} %bitcast.14), channel_id=1, replica_groups=mesh['seq'=64,'ch'=4] {'seq'}, dimensions={0} | all-to-all | bytes 524288 | tf_op jit(solution)/shard_map/all_to_all | solution.py:287
  54.9 1.3 %shard_map.150 = (bf16[512,128]{1,0:T(8,128)(2,1)S(1)}, f32[64,512]{1,0:T(8,128)S(1)}, bf16[64,512]{1,0:T(8,128)(2,1)S(1)}, bf16[64,512]{1,0:T(8,128)(2,1)S(1)},...) custom-call(s32[1]{0:T(128)} %bitcast.ch_ref.refs_0_, bf16[1024,128]{1,0:T(8,128)(2,1)S(1)} %bitcast.15, ...), custom_call_target="tpu_custom_call" | custom-call | tf_op jit(solution)/shard_map/pallas_call | solution.py:263
  56.2 12.6 %all_to_all.22 = bf16[64,8,128]{2,1,0:T(8,128)(2,1)S(1)} all-to-all(bf16[64,8,128]{2,1,0:T(8,128)(2,1)S(1)} %bitcast.19), channel_id=1, replica_groups=mesh['seq'=64,'ch'=4] {'seq'}, dimensions={0} | all-to-all | bytes 262144 | tf_op jit(solution)/shard_map/all_to_all | solution.py:287
  68.8 0.7 shard_map.151
  69.5 5.4 %all-to-all-start.3 = ((bf16[64,8,128]{2,1,0:T(8,128)(2,1)}), bf16[64,8,128]{2,1,0:T(8,128)(2,1)S(1)}, u32[]{:S(2)}, u32[]{:S(2)}) async-start(bf16[64,8,128]{2,1,0:T(8,128)(2,1)} %bitcast.9), calls=%async_computation.3 | async-start | bytes 262144 | tf_op jit(solution)/shard_map/all_to_all | solution.py:287
  74.9 2.3 %collective-permute-start.3 = (bf16[64,512]{1,0:T(8,128)(2,1)S(1)}, bf16[64,512]{1,0:T(8,128)(2,1)S(1)}, u32[]{:S(2)}, u32[]{:S(2)}) collective-permute-start(bf16[64,512]{1,0:T(8,128)(2,1)S(1)} %get-tuple-element.37), channel_id=1, source_target_pairs={{0,1},{1,2},{2,3},{3,0},{4,5},{5,6},{6,7},{7,4},{8,9},{9,10},{10,1... | collective-permute-start | bytes 196616 | tf_op jit(solution)/shard_map/ppermute | solution.py:291
  77.2 2.0 %collective-permute-start.4 = (bf16[64,512]{1,0:T(8,128)(2,1)S(1)}, bf16[64,512]{1,0:T(8,128)(2,1)S(1)}, u32[]{:S(2)}, u32[]{:S(2)}) collective-permute-start(bf16[64,512]{1,0:T(8,128)(2,1)S(1)} %get-tuple-element.38), channel_id=1, source_target_pairs={{0,3},{1,0},{2,1},{3,2},{4,7},{5,4},{6,5},{7,6},{8,11},{9,8},{10,9... | collective-permute-start | bytes 196616 | tf_op jit(solution)/shard_map/ppermute | solution.py:291
  79.1 5.1 %collective-permute-start.5 = (bf16[64,512]{1,0:T(8,128)(2,1)S(1)}, bf16[64,512]{1,0:T(8,128)(2,1)S(1)}, u32[]{:S(2)}, u32[]{:S(2)}) collective-permute-start(bf16[64,512]{1,0:T(8,128)(2,1)S(1)} %get-tuple-element.39), channel_id=1, source_target_pairs={{0,2},{1,3},{2,0},{3,1},{4,6},{5,7},{6,4},{7,5},{8,10},{9,11},{10,... | collective-permute-start | bytes 196616 | tf_op jit(solution)/shard_map/ppermute | solution.py:291
  84.2 0.0 collective-permute-done.3.came1_ref
  84.3 0.0 collective-permute-done.4.came3_ref
  84.3 4.8 %collective-permute-done.5.came2_ref = bf16[64,512]{1,0:T(8,128)(2,1)S(1)} collective-permute-done((bf16[64,512]{1,0:T(8,128)(2,1)S(1)}, bf16[64,512]{1,0:T(8,128)(2,1)S(1)}, u32[]{:S(2)}, u32[]{:S(2)}) %collective-permute-start.5) | collective-permute-done | bytes 65568 | tf_op jit(solution)/shard_map/ppermute | solution.py:291
  89.1 0.0 all-to-all-done.3
  89.1 0.7 shard_map.152
Async XLA Ops:
  1.5 13.8 %collective-permute-start.2 = (bf16[128,512]{1,0:T(8,128)(2,1)S(1)}, bf16[128,512]{1,0:T(8,128)(2,1)S(1)}, u32[]{:S(2)}, u32[]{:S(2)}) collective-permute-start(bf16[128,512]{1,0:T(8,128)(2,1)S(1)} %shard_map.146.own_ref), channel_id=1, source_target_pairs={{0,2},{1,3},{2,0},{3,1},{4,6},{5,7},{6,4},{7,5},{8,10},{9,11},{10,... | collective-permute-start | bytes 393224 | tf_op jit(solution)/shard_map/ppermute | solution.py:291
  7.9 11.3 %collective-permute-start.1 = (bf16[128,512]{1,0:T(8,128)(2,1)S(1)}, bf16[128,512]{1,0:T(8,128)(2,1)S(1)}, u32[]{:S(2)}, u32[]{:S(2)}) collective-permute-start(bf16[128,512]{1,0:T(8,128)(2,1)S(1)} %shard_map.146.own_ref), channel_id=1, source_target_pairs={{0,3},{1,0},{2,1},{3,2},{4,7},{5,4},{6,5},{7,6},{8,11},{9,8},{10,9... | collective-permute-start | bytes 393224 | tf_op jit(solution)/shard_map/ppermute | solution.py:291
  8.4 11.3 %collective-permute-start = (bf16[128,512]{1,0:T(8,128)(2,1)S(1)}, bf16[128,512]{1,0:T(8,128)(2,1)S(1)}, u32[]{:S(2)}, u32[]{:S(2)}) collective-permute-start(bf16[128,512]{1,0:T(8,128)(2,1)S(1)} %shard_map.146.own_ref), channel_id=1, source_target_pairs={{0,1},{1,2},{2,3},{3,0},{4,5},{5,6},{6,7},{7,4},{8,9},{9,10},{10,1... | collective-permute-start | bytes 393224 | tf_op jit(solution)/shard_map/ppermute | solution.py:291
  10.8 8.9 %copy-start = (bf16[256,256]{1,0:T(8,128)(2,1)S(1)}, bf16[256,256]{1,0:T(8,128)(2,1)}, u32[]{:S(2)}) copy-start(bf16[256,256]{1,0:T(8,128)(2,1)} %constant.18.clone.swap_ref.refs_2_) | copy-start | bytes 393220
  10.8 27.5 %copy-start.3 = (bf16[1024,256]{1,0:T(8,128)(2,1)S(1)}, bf16[1024,256]{1,0:T(8,128)(2,1)}, u32[]{:S(2)}) copy-start(bf16[1024,256]{1,0:T(8,128)(2,1)} %constant.14.clone.outer_ref) | copy-start | bytes 1572868
  19.7 18.6 %copy-start.1 = (bf16[512,512]{1,0:T(8,128)(2,1)S(1)}, bf16[512,512]{1,0:T(8,128)(2,1)}, u32[]{:S(2)}) copy-start(bf16[512,512]{1,0:T(8,128)(2,1)} %constant.16.clone.last_ref) | copy-start | bytes 1572868
  19.7 18.6 %copy-start.2 = (bf16[1024,256]{1,0:T(8,128)(2,1)S(1)}, bf16[1024,256]{1,0:T(8,128)(2,1)}, u32[]{:S(2)}) copy-start(bf16[1024,256]{1,0:T(8,128)(2,1)} %constant.15.clone.inner_ref) | copy-start | bytes 1572868
  69.5 19.6 %all-to-all-start.3 = ((bf16[64,8,128]{2,1,0:T(8,128)(2,1)}), bf16[64,8,128]{2,1,0:T(8,128)(2,1)S(1)}, u32[]{:S(2)}, u32[]{:S(2)}) async-start(bf16[64,8,128]{2,1,0:T(8,128)(2,1)} %bitcast.9), calls=%async_computation.3 | async-start | bytes 262144 | tf_op jit(solution)/shard_map/all_to_all | solution.py:287
  74.9 9.3 %collective-permute-start.3 = (bf16[64,512]{1,0:T(8,128)(2,1)S(1)}, bf16[64,512]{1,0:T(8,128)(2,1)S(1)}, u32[]{:S(2)}, u32[]{:S(2)}) collective-permute-start(bf16[64,512]{1,0:T(8,128)(2,1)S(1)} %get-tuple-element.37), channel_id=1, source_target_pairs={{0,1},{1,2},{2,3},{3,0},{4,5},{5,6},{6,7},{7,4},{8,9},{9,10},{10,1... | collective-permute-start | bytes 196616 | tf_op jit(solution)/shard_map/ppermute | solution.py:291
  77.2 7.1 %collective-permute-start.4 = (bf16[64,512]{1,0:T(8,128)(2,1)S(1)}, bf16[64,512]{1,0:T(8,128)(2,1)S(1)}, u32[]{:S(2)}, u32[]{:S(2)}) collective-permute-start(bf16[64,512]{1,0:T(8,128)(2,1)S(1)} %get-tuple-element.38), channel_id=1, source_target_pairs={{0,3},{1,0},{2,1},{3,2},{4,7},{5,4},{6,5},{7,6},{8,11},{9,8},{10,9... | collective-permute-start | bytes 196616 | tf_op jit(solution)/shard_map/ppermute | solution.py:291
  79.1 9.9 %collective-permute-start.5 = (bf16[64,512]{1,0:T(8,128)(2,1)S(1)}, bf16[64,512]{1,0:T(8,128)(2,1)S(1)}, u32[]{:S(2)}, u32[]{:S(2)}) collective-permute-start(bf16[64,512]{1,0:T(8,128)(2,1)S(1)} %get-tuple-element.39), channel_id=1, source_target_pairs={{0,2},{1,3},{2,0},{3,1},{4,6},{5,7},{6,4},{7,5},{8,10},{9,11},{10,... | collective-permute-start | bytes 196616 | tf_op jit(solution)/shard_map/ppermute | solution.py:291

commit v3 on v2

--- a/solution.py
+++ b/solution.py
@@ -129,7 +129,7 @@
 ):
     ch = ch_ref[0]
     for shift, ref in ((0, own_ref), (1, got1_ref), (3, got3_ref), (2, got2_ref)):
-        at = pl.multiple_of(lax.rem(ch + (4 - shift), 4) * 64, 64)
+        at = pl.multiple_of((ch ^ shift) * 64, 64)
         in_ref[pl.ds(at, 64), :] = ref[:64, :]
         grad_ref[pl.ds(at, 64), :] = ref[64:, :]
     full_in = in_ref[...]
@@ -204,7 +204,7 @@
     ch = ch_ref[0]
 
     def block(shift):
-        at = pl.multiple_of(lax.rem(ch + shift, 4) * 64, 64)
+        at = pl.multiple_of((ch ^ shift) * 64, 64)
         return part_ref[pl.ds(at, 64), :]
 
     own_ref[...] = block(0)
@@ -288,7 +288,7 @@
 
 
 def shifted(value, shift):
-    return lax.ppermute(value, "ch", [(i, (i + shift) % 4) for i in range(4)])
+    return lax.ppermute(value, "ch", [(i, i ^ shift) for i in range(4)])
 
 
 def on_device(inputs, w_value, w_gate, w_out, filter_taps, grad_out):
@@ -303,7 +303,8 @@
     rows, length = inputs.shape
     (own,) = copied(pack_kernel, [inside((2 * rows, length), inputs.dtype)], inputs, grad_out)
     later = (w_value.T, w_gate.T, w_out, filter_taps, twiddle)
-    got = [shifted(own, s) for s in (1, 3, 2)]
+    got = [shifted(own, s) for s in (1, 3)]
+    got.append(shifted(own, 2))
     wv, wg, wo, taps, tw = copied(fetch_kernel, [inside(x.shape, x.dtype) for x in later], *later)
     msg, gate, d_gated, full_in, full_grad = call(
         project_kernel,
@@ -334,13 +335,13 @@
         scalar=ch, scratch=[pltpu.VMEM((256, 512), F32)],
     )
     arrived = exchanged(sums, "seq")
-    came2, came1 = shifted(send2, 2), shifted(send1, 1)
+    came3, came1 = shifted(send3, 3), shifted(send1, 1)
     total = call(
         lambda *refs: total_kernel(*refs, scale=scale),
         inside((512, LANES), BF16), arrived,
     )
     spread = exchanged(total, "seq")
-    came3 = shifted(send3, 3)
+    came2 = shifted(send2, 2)
     d_inputs, dwv, dwg, dwo = call(
         settle_kernel,
         [outside((64, 512), BF16)] + [outside((64, 256), F32)] * 3,

time: 90.1 us -> 90.7 us (level)
  waiting for transfers between devices: 12.6 us -> 17.3 us
  starting transfers between devices: 24 us -> 19.9 us
    ppermute x6, waiting for transfers between devices: 12.6 us -> 17.3 us  [shifted(): return lax.ppermute(value, 'ch', [(i, i ^ shift) for i in range(4)])]
    ppermute x6, starting transfers between devices: 18.6 us -> 14.4 us  [shifted(): return lax.ppermute(value, 'ch', [(i, i ^ shift) for i in range(4)])]
where the time goes in v3:
time: 90.7 us; the launch traced here: 90.2 us
  blocking collectives  44.5 us (49%)
  starting transfers between devices  19.9 us (22%)
  waiting for transfers between devices  17.3 us (19%)
  Pallas kernels  7.81 us (9%)
    all_to_all x3, blocking collectives, exchanged(): return lax.all_to_all(parts, axis, 0, 0, tiled=True).reshape(rows.shape)  44.5 us
    ppermute x6, waiting for transfers between devices, shifted(): return lax.ppermute(value, 'ch', [(i, i ^ shift) for i in range(4)])  17.3 us
    ppermute x6, starting transfers between devices, shifted(): return lax.ppermute(value, 'ch', [(i, i ^ shift) for i in range(4)])  14.4 us
    pallas_call x5, Pallas kernels, call(): pl.pallas_call(kernel, out_shape=tuple(outs) if many else outs, in_specs=...  5.78 us
    all_to_all x1, starting transfers between devices, exchanged(): return lax.all_to_all(parts, axis, 0, 0, tiled=True).reshape(rows.shape)  5.42 us
    pallas_call x2, Pallas kernels, copied(): pl.pallas_call(kernel, out_shape=tuple(outs), in_specs=[ANY] * len(args),...  2.03 us
  transfers between devices with their start and end apart: 7, of which 4 were waited for; matrix products, arithmetic and copies ran while one was open for 0% of the time, Pallas kernels for 1%

profile of v3, /device:TPU:32, one launch (start us, length us, event | category | flops | bytes accessed | tf_op | source)
XLA Modules:
  0.0 90.2 jit_solution(10892723050580998854)
XLA Ops:
  0.6 0.9 shard_map.146.own_ref
  1.5 6.4 %collective-permute-start.2 = (bf16[128,512]{1,0:T(8,128)(2,1)S(1)}, bf16[128,512]{1,0:T(8,128)(2,1)S(1)}, u32[]{:S(2)}, u32[]{:S(2)}) collective-permute-start(bf16[128,512]{1,0:T(8,128)(2,1)S(1)} %shard_map.146.own_ref), channel_id=1, source_target_pairs={{0,2},{1,3},{2,0},{3,1},{4,6},{5,7},{6,4},{7,5},{8,10},{9,11},{10,... | collective-permute-start | bytes 393224 | tf_op jit(solution)/shard_map/ppermute | solution.py:291
  7.9 0.6 collective-permute-start.1
  8.4 0.9 %collective-permute-start = (bf16[128,512]{1,0:T(8,128)(2,1)S(1)}, bf16[128,512]{1,0:T(8,128)(2,1)S(1)}, u32[]{:S(2)}, u32[]{:S(2)}) collective-permute-start(bf16[128,512]{1,0:T(8,128)(2,1)S(1)} %shard_map.146.own_ref), channel_id=1, source_target_pairs={{0,1},{1,0},{2,3},{3,2},{4,5},{5,4},{6,7},{7,6},{8,9},{9,8},{10,11... | collective-permute-start | bytes 393224 | tf_op jit(solution)/shard_map/ppermute | solution.py:291
  9.4 0.0 copy-start
  9.4 0.0 copy-start.3
  9.4 1.1 %shard_map.147 = (bf16[64,256]{1,0:T(8,128)(2,1)S(1)}, bf16[64,256]{1,0:T(8,128)(2,1)S(1)}, bf16[64,256]{1,0:T(8,128)(2,1)S(1)}, f32[64,512]{1,0:T(8,128)S(1)}, f32[2,256,128]{2,1,0:T(8,128)S(1)}) custom-call(bf16[64,256]{1,0:T(8,128)(2,1)} %bitcast.20, bf16[64,256]{1,0:T(8,128)(2,1)} %bitcast.21, bf16[64,256]{1,0:T(8,128)(2,1)} %refs_2_.2, ...), custom_call_target="tpu_custom_call" | custom-call | tf_op jit(solution)/shard_map/pallas_call | solution.py:274
  10.5 4.3 %collective-permute-done.2.got2_ref = bf16[128,512]{1,0:T(8,128)(2,1)S(1)} collective-permute-done((bf16[128,512]{1,0:T(8,128)(2,1)S(1)}, bf16[128,512]{1,0:T(8,128)(2,1)S(1)}, u32[]{:S(2)}, u32[]{:S(2)}) %collective-permute-start.2) | collective-permute-done | bytes 131104 | tf_op jit(solution)/shard_map/ppermute | solution.py:291
  14.8 4.9 %collective-permute-done.1.got3_ref = bf16[128,512]{1,0:T(8,128)(2,1)S(1)} collective-permute-done((bf16[128,512]{1,0:T(8,128)(2,1)S(1)}, bf16[128,512]{1,0:T(8,128)(2,1)S(1)}, u32[]{:S(2)}, u32[]{:S(2)}) %collective-permute-start.1) | collective-permute-done | bytes 131104 | tf_op jit(solution)/shard_map/ppermute | solution.py:291
  19.7 0.0 collective-permute-done.got1_ref
  19.7 0.0 copy-done
  19.7 0.0 copy-start.1
  19.7 0.0 copy-start.2
  19.8 0.6 shard_map.148
  20.3 18.0 %all_to_all.20 = bf16[64,16,128]{2,1,0:T(8,128)(2,1)S(1)} all-to-all(bf16[64,16,128]{2,1,0:T(8,128)(2,1)S(1)} %bitcast.18), channel_id=1, replica_groups=mesh['seq'=64,'ch'=4] {'seq'}, dimensions={0} | all-to-all | bytes 524288 | tf_op jit(solution)/shard_map/all_to_all | solution.py:287
  38.3 0.0 copy-done.3
  38.3 0.0 copy-done.1
  38.3 0.0 copy-done.2
  38.3 2.6 %shard_map.149 = bf16[1024,128]{1,0:T(8,128)(2,1)S(1)} custom-call(bf16[1024,128]{1,0:T(8,128)(2,1)S(1)} %bitcast.13, bf16[256,256]{1,0:T(8,128)(2,1)S(1)} %copy-done, bf16[1024,256]{1,0:T(8,128)(2,1)S(1)} %copy-done.3, bf16[1024,256]{1,0:T(8,128)(2,1)S(1)} %copy-done.2, bf16[512,512]{1,0:T(8,128)(2,1)S(1)} %copy-done.1, ...), custom_call_target="tpu_custom_call" | custom-call | tf_op jit(solution)/shard_map/pallas_call | solution.py:263
  40.9 14.0 %all_to_all.21 = bf16[64,16,128]{2,1,0:T(8,128)(2,1)S(1)} all-to-all(bf16[64,16,128]{2,1,0:T(8,128)(2,1)S(1)} %bitcast.14), channel_id=1, replica_groups=mesh['seq'=64,'ch'=4] {'seq'}, dimensions={0} | all-to-all | bytes 524288 | tf_op jit(solution)/shard_map/all_to_all | solution.py:287
  54.9 1.2 %shard_map.150 = (bf16[512,128]{1,0:T(8,128)(2,1)S(1)}, f32[64,512]{1,0:T(8,128)S(1)}, bf16[64,512]{1,0:T(8,128)(2,1)S(1)}, bf16[64,512]{1,0:T(8,128)(2,1)S(1)},...) custom-call(s32[1]{0:T(128)} %bitcast.ch_ref.refs_0_, bf16[1024,128]{1,0:T(8,128)(2,1)S(1)} %bitcast.15, ...), custom_call_target="tpu_custom_call" | custom-call | tf_op jit(solution)/shard_map/pallas_call | solution.py:263
  56.1 12.6 %all_to_all.22 = bf16[64,8,128]{2,1,0:T(8,128)(2,1)S(1)} all-to-all(bf16[64,8,128]{2,1,0:T(8,128)(2,1)S(1)} %bitcast.19), channel_id=1, replica_groups=mesh['seq'=64,'ch'=4] {'seq'}, dimensions={0} | all-to-all | bytes 262144 | tf_op jit(solution)/shard_map/all_to_all | solution.py:287
  68.6 0.7 shard_map.151
  69.4 5.4 %all-to-all-start.3 = ((bf16[64,8,128]{2,1,0:T(8,128)(2,1)}), bf16[64,8,128]{2,1,0:T(8,128)(2,1)S(1)}, u32[]{:S(2)}, u32[]{:S(2)}) async-start(bf16[64,8,128]{2,1,0:T(8,128)(2,1)} %bitcast.9), calls=%async_computation.3 | async-start | bytes 262144 | tf_op jit(solution)/shard_map/all_to_all | solution.py:287
  74.8 2.2 %collective-permute-start.3 = (bf16[64,512]{1,0:T(8,128)(2,1)S(1)}, bf16[64,512]{1,0:T(8,128)(2,1)S(1)}, u32[]{:S(2)}, u32[]{:S(2)}) collective-permute-start(bf16[64,512]{1,0:T(8,128)(2,1)S(1)} %get-tuple-element.37), channel_id=1, source_target_pairs={{0,1},{1,0},{2,3},{3,2},{4,5},{5,4},{6,7},{7,6},{8,9},{9,8},{10,11... | collective-permute-start | bytes 196616 | tf_op jit(solution)/shard_map/ppermute | solution.py:291
  77.1 3.1 %collective-permute-start.4 = (bf16[64,512]{1,0:T(8,128)(2,1)S(1)}, bf16[64,512]{1,0:T(8,128)(2,1)S(1)}, u32[]{:S(2)}, u32[]{:S(2)}) collective-permute-start(bf16[64,512]{1,0:T(8,128)(2,1)S(1)} %get-tuple-element.38), channel_id=1, source_target_pairs={{0,3},{1,2},{2,1},{3,0},{4,7},{5,6},{6,5},{7,4},{8,11},{9,10},{10,... | collective-permute-start | bytes 196616 | tf_op jit(solution)/shard_map/ppermute | solution.py:291
  80.2 1.2 %collective-permute-start.5 = (bf16[64,512]{1,0:T(8,128)(2,1)S(1)}, bf16[64,512]{1,0:T(8,128)(2,1)S(1)}, u32[]{:S(2)}, u32[]{:S(2)}) collective-permute-start(bf16[64,512]{1,0:T(8,128)(2,1)S(1)} %get-tuple-element.39), channel_id=1, source_target_pairs={{0,2},{1,3},{2,0},{3,1},{4,6},{5,7},{6,4},{7,5},{8,10},{9,11},{10,... | collective-permute-start | bytes 196616 | tf_op jit(solution)/shard_map/ppermute | solution.py:291
  81.4 0.0 collective-permute-done.3.came1_ref
  81.4 2.7 %collective-permute-done.4.came3_ref = bf16[64,512]{1,0:T(8,128)(2,1)S(1)} collective-permute-done((bf16[64,512]{1,0:T(8,128)(2,1)S(1)}, bf16[64,512]{1,0:T(8,128)(2,1)S(1)}, u32[]{:S(2)}, u32[]{:S(2)}) %collective-permute-start.4) | collective-permute-done | bytes 65568 | tf_op jit(solution)/shard_map/ppermute | solution.py:291
  84.1 5.4 %collective-permute-done.5.came2_ref = bf16[64,512]{1,0:T(8,128)(2,1)S(1)} collective-permute-done((bf16[64,512]{1,0:T(8,128)(2,1)S(1)}, bf16[64,512]{1,0:T(8,128)(2,1)S(1)}, u32[]{:S(2)}, u32[]{:S(2)}) %collective-permute-start.5) | collective-permute-done | bytes 65568 | tf_op jit(solution)/shard_map/ppermute | solution.py:291
  89.5 0.0 all-to-all-done.3
  89.5 0.7 shard_map.152
Async XLA Ops:
  1.5 13.3 %collective-permute-start.2 = (bf16[128,512]{1,0:T(8,128)(2,1)S(1)}, bf16[128,512]{1,0:T(8,128)(2,1)S(1)}, u32[]{:S(2)}, u32[]{:S(2)}) collective-permute-start(bf16[128,512]{1,0:T(8,128)(2,1)S(1)} %shard_map.146.own_ref), channel_id=1, source_target_pairs={{0,2},{1,3},{2,0},{3,1},{4,6},{5,7},{6,4},{7,5},{8,10},{9,11},{10,... | collective-permute-start | bytes 393224 | tf_op jit(solution)/shard_map/ppermute | solution.py:291
  7.9 11.8 %collective-permute-start.1 = (bf16[128,512]{1,0:T(8,128)(2,1)S(1)}, bf16[128,512]{1,0:T(8,128)(2,1)S(1)}, u32[]{:S(2)}, u32[]{:S(2)}) collective-permute-start(bf16[128,512]{1,0:T(8,128)(2,1)S(1)} %shard_map.146.own_ref), channel_id=1, source_target_pairs={{0,3},{1,2},{2,1},{3,0},{4,7},{5,6},{6,5},{7,4},{8,11},{9,10},{10,... | collective-permute-start | bytes 393224 | tf_op jit(solution)/shard_map/ppermute | solution.py:291
  8.4 11.3 %collective-permute-start = (bf16[128,512]{1,0:T(8,128)(2,1)S(1)}, bf16[128,512]{1,0:T(8,128)(2,1)S(1)}, u32[]{:S(2)}, u32[]{:S(2)}) collective-permute-start(bf16[128,512]{1,0:T(8,128)(2,1)S(1)} %shard_map.146.own_ref), channel_id=1, source_target_pairs={{0,1},{1,0},{2,3},{3,2},{4,5},{5,4},{6,7},{7,6},{8,9},{9,8},{10,11... | collective-permute-start | bytes 393224 | tf_op jit(solution)/shard_map/ppermute | solution.py:291
  9.4 10.4 %copy-start = (bf16[256,256]{1,0:T(8,128)(2,1)S(1)}, bf16[256,256]{1,0:T(8,128)(2,1)}, u32[]{:S(2)}) copy-start(bf16[256,256]{1,0:T(8,128)(2,1)} %constant.18.clone.swap_ref.refs_2_) | copy-start | bytes 393220
  9.4 28.9 %copy-start.3 = (bf16[1024,256]{1,0:T(8,128)(2,1)S(1)}, bf16[1024,256]{1,0:T(8,128)(2,1)}, u32[]{:S(2)}) copy-start(bf16[1024,256]{1,0:T(8,128)(2,1)} %constant.14.clone.outer_ref) | copy-start | bytes 1572868
  19.7 18.6 %copy-start.1 = (bf16[512,512]{1,0:T(8,128)(2,1)S(1)}, bf16[512,512]{1,0:T(8,128)(2,1)}, u32[]{:S(2)}) copy-start(bf16[512,512]{1,0:T(8,128)(2,1)} %constant.16.clone.last_ref) | copy-start | bytes 1572868
  19.7 18.6 %copy-start.2 = (bf16[1024,256]{1,0:T(8,128)(2,1)S(1)}, bf16[1024,256]{1,0:T(8,128)(2,1)}, u32[]{:S(2)}) copy-start(bf16[1024,256]{1,0:T(8,128)(2,1)} %constant.15.clone.inner_ref) | copy-start | bytes 1572868
  69.4 20.1 %all-to-all-start.3 = ((bf16[64,8,128]{2,1,0:T(8,128)(2,1)}), bf16[64,8,128]{2,1,0:T(8,128)(2,1)S(1)}, u32[]{:S(2)}, u32[]{:S(2)}) async-start(bf16[64,8,128]{2,1,0:T(8,128)(2,1)} %bitcast.9), calls=%async_computation.3 | async-start | bytes 262144 | tf_op jit(solution)/shard_map/all_to_all | solution.py:287
  74.8 6.6 %collective-permute-start.3 = (bf16[64,512]{1,0:T(8,128)(2,1)S(1)}, bf16[64,512]{1,0:T(8,128)(2,1)S(1)}, u32[]{:S(2)}, u32[]{:S(2)}) collective-permute-start(bf16[64,512]{1,0:T(8,128)(2,1)S(1)} %get-tuple-element.37), channel_id=1, source_target_pairs={{0,1},{1,0},{2,3},{3,2},{4,5},{5,4},{6,7},{7,6},{8,9},{9,8},{10,11... | collective-permute-start | bytes 196616 | tf_op jit(solution)/shard_map/ppermute | solution.py:291
  77.1 7.0 %collective-permute-start.4 = (bf16[64,512]{1,0:T(8,128)(2,1)S(1)}, bf16[64,512]{1,0:T(8,128)(2,1)S(1)}, u32[]{:S(2)}, u32[]{:S(2)}) collective-permute-start(bf16[64,512]{1,0:T(8,128)(2,1)S(1)} %get-tuple-element.38), channel_id=1, source_target_pairs={{0,3},{1,2},{2,1},{3,0},{4,7},{5,6},{6,5},{7,4},{8,11},{9,10},{10,... | collective-permute-start | bytes 196616 | tf_op jit(solution)/shard_map/ppermute | solution.py:291
  80.2 9.3 %collective-permute-start.5 = (bf16[64,512]{1,0:T(8,128)(2,1)S(1)}, bf16[64,512]{1,0:T(8,128)(2,1)S(1)}, u32[]{:S(2)}, u32[]{:S(2)}) collective-permute-start(bf16[64,512]{1,0:T(8,128)(2,1)S(1)} %get-tuple-element.39), channel_id=1, source_target_pairs={{0,2},{1,3},{2,0},{3,1},{4,6},{5,7},{6,4},{7,5},{8,10},{9,11},{10,... | collective-permute-start | bytes 196616 | tf_op jit(solution)/shard_map/ppermute | solution.py:291

commit v4 on v3

--- a/solution.py
+++ b/solution.py
@@ -150,7 +150,9 @@
     return dot_right(z, table_high, table_low)
 
 
-def convolve_kernel(got_ref, swap_ref, outer_ref, inner_ref, last_ref, tw_ref, out_ref):
+def convolve_kernel(
+    got_ref, swap_ref, half_swap_ref, outer_ref, inner_ref, last_ref, tw_ref, out_ref, filt_ref
+):
     rows = outer_ref.shape[0] // 2
     size = 2 * LANES
     ih, il, jh, jl = (inner_ref[k * size : (k + 1) * size, :] for k in range(4))
@@ -175,27 +177,31 @@
         b = jnp.concatenate([re * tw_re + im * tw_im, im * tw_re - re * tw_im], axis=0)
         back.append(dot_left(last_ref[: rows // 2, :], last_ref[rows // 2 :, :], b))
     mixed, d_value, d_filter = back
-    signals = (mixed.astype(BF16), d_value.astype(BF16), *split_up(d_filter))
-    blocks = [[x[g * 64 : (g + 1) * 64] for x in signals] for g in range(64 // GROUP)]
-    write_messages(out_ref, swap_ref[...], blocks)
+    swap = half_swap_ref[...]
+    for ref, signals in (
+        (out_ref, (mixed.astype(BF16), d_value.astype(BF16))),
+        (filt_ref, split_up(d_filter)),
+    ):
+        blocks = [[x[g * 64 : (g + 1) * 64] for x in signals] for g in range(64 // GROUP)]
+        write_messages(ref, swap, blocks)
+
+
+def received_signal(groups, k):
+    cols = []
+    for u in range(4):
+        at = (k * 4 + u) * GROUP
+        cols.append(jnp.concatenate([x[at : at + GROUP] for x in groups], axis=0))
+    return jnp.concatenate(cols, axis=1)
 
 
 def gradient_kernel(
-    ch_ref, got_ref, swap_ref, gate_ref, dgated_ref, in_ref, grad_ref, wv_ref, wg_ref,
-    sums_ref, own_ref, send1_ref, send3_ref, send2_ref, filt_ref, part_ref, *, scale
+    ch_ref, got_ref, taps_ref, swap_ref, gate_ref, dgated_ref, in_ref, grad_ref, wv_ref, wg_ref,
+    sums_ref, own_ref, send1_ref, send3_ref, send2_ref, part_ref
 ):
     groups = read_messages(got_ref, swap_ref[...])
 
-    def signal(k):
-        cols = []
-        for u in range(4):
-            at = (k * 4 + u) * GROUP
-            cols.append(jnp.concatenate([x[at : at + GROUP] for x in groups], axis=0))
-        return jnp.concatenate(cols, axis=1)
-
-    mixed = signal(0).astype(F32)
-    d_value = signal(1)
-    filt_ref[...] = (signal(2).astype(F32) + signal(3).astype(F32)) * scale
+    mixed = received_signal(groups, 0).astype(F32)
+    d_value = received_signal(groups, 1)
     gated_out = (gate_ref[...] * mixed).astype(BF16)
     d_gate = (dgated_ref[...] * mixed).astype(BF16)
     both = jnp.concatenate([d_value, d_gate], axis=0)
@@ -218,13 +224,22 @@
         for a in range(value.shape[0] // 8):
             tiles += lane_blocks(value[8 * a : 8 * a + 8])
     tiles += [jnp.zeros_like(tiles[0])] * (64 - len(tiles))
-    sums_ref[...] = jnp.concatenate(tiles, axis=0).astype(BF16)
+    taps = taps_ref[...].astype(F32)
+    rows = [x for i, tile in enumerate(tiles) for x in (tile, taps[8 * i : 8 * i + 8])]
+    sums_ref[...] = jnp.concatenate(rows, axis=0).astype(BF16)
 
 
 def total_kernel(got_ref, out_ref, *, scale):
-    total = got_ref[...].astype(F32).reshape(64, 8, LANES).sum(axis=0) * scale
+    got = got_ref[...].astype(F32).reshape(64, 16, LANES)
+    total = got[:, :8].sum(axis=0) * scale
     whole = jnp.broadcast_to(total[None], (64, 8, LANES)).reshape(512, LANES)
     out_ref[...] = whole.astype(BF16)
+
+
+def taps_kernel(got_ref, swap_ref, filt_ref, *, scale):
+    groups = read_messages(got_ref, swap_ref[...])
+    high, low = received_signal(groups, 2), received_signal(groups, 3)
+    filt_ref[...] = (high.astype(F32) + low.astype(F32)) * scale
 
 
 def settle_kernel(
@@ -296,6 +311,7 @@
     scale = 1.0 / math.sqrt(tokens)
     outer, inner, last, twiddle = [jnp.asarray(t) for t in transform_tables(tokens)]
     swap = jnp.asarray(exchange_table(16))
+    half_swap = jnp.asarray(exchange_table(8))
     ch = lax.axis_index("ch").astype(jnp.int32).reshape(1)
     inside = pltpu.VMEM
     outside = jax.ShapeDtypeStruct
@@ -317,21 +333,20 @@
         ],
         own, *got, wv, wg, wo, taps, swap, scalar=ch,
     )
-    back = call(
-        convolve_kernel, inside((1024, LANES), BF16),
-        exchanged(msg, "seq"), swap, outer, inner, last, tw,
-    )
-    sums, mine, send1, send3, send2, d_filter = call(
-        lambda *refs: gradient_kernel(*refs, scale=scale),
+    back, taps_back = call(
+        convolve_kernel, [inside((512, LANES), BF16)] * 2,
+        exchanged(msg, "seq"), swap, half_swap, outer, inner, last, tw,
+    )
+    sums, mine, send1, send3, send2 = call(
+        gradient_kernel,
         [
-            inside((512, LANES), BF16),
+            inside((1024, LANES), BF16),
             inside((64, 512), F32),
             inside((64, 512), BF16),
             inside((64, 512), BF16),
             inside((64, 512), BF16),
-            outside((64, 512), F32),
         ],
-        exchanged(back, "seq"), swap, gate, d_gated, full_in, full_grad, wv, wg,
+        exchanged(back, "seq"), taps_back, half_swap, gate, d_gated, full_in, full_grad, wv, wg,
         scalar=ch, scratch=[pltpu.VMEM((256, 512), F32)],
     )
     arrived = exchanged(sums, "seq")
@@ -342,6 +357,10 @@
     )
     spread = exchanged(total, "seq")
     came2 = shifted(send2, 2)
+    d_filter = call(
+        lambda *refs: taps_kernel(*refs, scale=scale),
+        outside((64, 512), F32), arrived, swap,
+    )
     d_inputs, dwv, dwg, dwo = call(
         settle_kernel,
         [outside((64, 512), BF16)] + [outside((64, 256), F32)] * 3,

time: 90.7 us -> 89.9 us (level)
  waiting for transfers between devices: 17.3 us -> 16.3 us
    ppermute x6, waiting for transfers between devices: 17.3 us -> 16.3 us  [shifted(): return lax.ppermute(value, 'ch', [(i, i ^ shift) for i in range(4)])]
    pallas_call x5 -> x6, Pallas kernels: 5.78 us -> 6 us  [call(): pl.pallas_call(kernel, out_shape=tuple(outs) if many else outs, in_specs=...]
  transfers between devices with their start and end apart: 7 -> 7, of which waited for: 4 -> 4; matrix products, arithmetic and copies ran while one was open for 0% -> 0% of each run, Pallas kernels for 1% -> 2%
where the time goes in v4:
time: 89.9 us; the launch traced here: 89.4 us
  blocking collectives  44.6 us (50%)
  starting transfers between devices  19.7 us (22%)
  waiting for transfers between devices  16.3 us (18%)
  Pallas kernels  8.02 us (9%)
    all_to_all x3, blocking collectives, exchanged(): return lax.all_to_all(parts, axis, 0, 0, tiled=True).reshape(rows.shape)  44.6 us
    ppermute x6, waiting for transfers between devices, shifted(): return lax.ppermute(value, 'ch', [(i, i ^ shift) for i in range(4)])  16.3 us
    ppermute x6, starting transfers between devices, shifted(): return lax.ppermute(value, 'ch', [(i, i ^ shift) for i in range(4)])  14.4 us
    pallas_call x6, Pallas kernels, call(): pl.pallas_call(kernel, out_shape=tuple(outs) if many else outs, in_specs=...  6 us
    all_to_all x1, starting transfers between devices, exchanged(): return lax.all_to_all(parts, axis, 0, 0, tiled=True).reshape(rows.shape)  5.28 us
    pallas_call x2, Pallas kernels, copied(): pl.pallas_call(kernel, out_shape=tuple(outs), in_specs=[ANY] * len(args),...  2.03 us
  transfers between devices with their start and end apart: 7, of which 4 were waited for; matrix products, arithmetic and copies ran while one was open for 0% of the time, Pallas kernels for 2%

profile of v4, /device:TPU:32, one launch (start us, length us, event | category | flops | bytes accessed | tf_op | source)
XLA Modules:
  0.0 89.4 jit_solution(3821705528217852779)
XLA Ops:
  0.6 0.9 shard_map.155.own_ref
  1.5 6.4 %collective-permute-start.2 = (bf16[128,512]{1,0:T(8,128)(2,1)S(1)}, bf16[128,512]{1,0:T(8,128)(2,1)S(1)}, u32[]{:S(2)}, u32[]{:S(2)}) collective-permute-start(bf16[128,512]{1,0:T(8,128)(2,1)S(1)} %shard_map.155.own_ref), channel_id=1, source_target_pairs={{0,2},{1,3},{2,0},{3,1},{4,6},{5,7},{6,4},{7,5},{8,10},{9,11},{10,... | collective-permute-start | bytes 393224 | tf_op jit(solution)/shard_map/ppermute | solution.py:306
  7.9 0.6 collective-permute-start.1
  8.4 0.9 %collective-permute-start = (bf16[128,512]{1,0:T(8,128)(2,1)S(1)}, bf16[128,512]{1,0:T(8,128)(2,1)S(1)}, u32[]{:S(2)}, u32[]{:S(2)}) collective-permute-start(bf16[128,512]{1,0:T(8,128)(2,1)S(1)} %shard_map.155.own_ref), channel_id=1, source_target_pairs={{0,1},{1,0},{2,3},{3,2},{4,5},{5,4},{6,7},{7,6},{8,9},{9,8},{10,11... | collective-permute-start | bytes 393224 | tf_op jit(solution)/shard_map/ppermute | solution.py:306
  9.4 1.1 %shard_map.156 = (bf16[64,256]{1,0:T(8,128)(2,1)S(1)}, bf16[64,256]{1,0:T(8,128)(2,1)S(1)}, bf16[64,256]{1,0:T(8,128)(2,1)S(1)}, f32[64,512]{1,0:T(8,128)S(1)}, f32[2,256,128]{2,1,0:T(8,128)S(1)}) custom-call(bf16[64,256]{1,0:T(8,128)(2,1)} %bitcast.21, bf16[64,256]{1,0:T(8,128)(2,1)} %bitcast.22, bf16[64,256]{1,0:T(8,128)(2,1)} %refs_2_.1, ...), custom_call_target="tpu_custom_call" | custom-call | tf_op jit(solution)/shard_map/pallas_call | solution.py:289
  10.5 4.3 %collective-permute-done.2.got2_ref = bf16[128,512]{1,0:T(8,128)(2,1)S(1)} collective-permute-done((bf16[128,512]{1,0:T(8,128)(2,1)S(1)}, bf16[128,512]{1,0:T(8,128)(2,1)S(1)}, u32[]{:S(2)}, u32[]{:S(2)}) %collective-permute-start.2) | collective-permute-done | bytes 131104 | tf_op jit(solution)/shard_map/ppermute | solution.py:306
  14.8 4.9 %collective-permute-done.1.got3_ref = bf16[128,512]{1,0:T(8,128)(2,1)S(1)} collective-permute-done((bf16[128,512]{1,0:T(8,128)(2,1)S(1)}, bf16[128,512]{1,0:T(8,128)(2,1)S(1)}, u32[]{:S(2)}, u32[]{:S(2)}) %collective-permute-start.1) | collective-permute-done | bytes 131104 | tf_op jit(solution)/shard_map/ppermute | solution.py:306
  19.7 0.0 collective-permute-done.got1_ref
  19.7 0.0 copy-done
  19.7 0.0 copy-start.2
  19.8 0.6 shard_map.157
  20.3 0.0 copy-start.4
  20.3 18.0 %all_to_all.20 = bf16[64,16,128]{2,1,0:T(8,128)(2,1)S(1)} all-to-all(bf16[64,16,128]{2,1,0:T(8,128)(2,1)S(1)} %bitcast.19), channel_id=1, replica_groups=mesh['seq'=64,'ch'=4] {'seq'}, dimensions={0} | all-to-all | bytes 524288 | tf_op jit(solution)/shard_map/all_to_all | solution.py:302
  38.3 0.0 copy-done.3
  38.3 0.0 copy-done.1
  38.3 0.0 copy-done.2
  38.3 0.0 copy-done.4
  38.3 2.5 %shard_map.158 = (bf16[512,128]{1,0:T(8,128)(2,1)S(1)}, bf16[512,128]{1,0:T(8,128)(2,1)S(1)}) custom-call(bf16[1024,128]{1,0:T(8,128)(2,1)S(1)} %bitcast.15, bf16[256,256]{1,0:T(8,128)(2,1)S(1)} %copy-done, bf16[128,128]{1,0:T(8,128)(2,1)S(1)} %copy-done.4, bf16[1024,256]{1,0:T(8,128)(2,1)S(1)} %copy-done.3, bf16[1024,256]{1,0:T(8,128)(2,1)S(1)} %copy-done.2, ...), custom_call_target="tpu_custom_call" | custom-call | tf_op jit(solution)/shard_map/pallas_call | solution.py:278
  40.8 12.6 %all_to_all.21 = bf16[64,8,128]{2,1,0:T(8,128)(2,1)S(1)} all-to-all(bf16[64,8,128]{2,1,0:T(8,128)(2,1)S(1)} %bitcast.20), channel_id=1, replica_groups=mesh['seq'=64,'ch'=4] {'seq'}, dimensions={0} | all-to-all | bytes 262144 | tf_op jit(solution)/shard_map/all_to_all | solution.py:302
  53.4 0.5 shard_map.159
  53.9 14.0 %all_to_all.22 = bf16[64,16,128]{2,1,0:T(8,128)(2,1)S(1)} all-to-all(bf16[64,16,128]{2,1,0:T(8,128)(2,1)S(1)} %bitcast.18), channel_id=1, replica_groups=mesh['seq'=64,'ch'=4] {'seq'}, dimensions={0} | all-to-all | bytes 524288 | tf_op jit(solution)/shard_map/all_to_all | solution.py:302
  68.0 0.7 shard_map.160
  68.7 5.3 %all-to-all-start.3 = ((bf16[64,8,128]{2,1,0:T(8,128)(2,1)}), bf16[64,8,128]{2,1,0:T(8,128)(2,1)S(1)}, u32[]{:S(2)}, u32[]{:S(2)}) async-start(bf16[64,8,128]{2,1,0:T(8,128)(2,1)} %bitcast.9), calls=%async_computation.3 | async-start | bytes 262144 | tf_op jit(solution)/shard_map/all_to_all | solution.py:302
  74.0 2.2 %collective-permute-start.3 = (bf16[64,512]{1,0:T(8,128)(2,1)S(1)}, bf16[64,512]{1,0:T(8,128)(2,1)S(1)}, u32[]{:S(2)}, u32[]{:S(2)}) collective-permute-start(bf16[64,512]{1,0:T(8,128)(2,1)S(1)} %get-tuple-element.40), channel_id=1, source_target_pairs={{0,1},{1,0},{2,3},{3,2},{4,5},{5,4},{6,7},{7,6},{8,9},{9,8},{10,11... | collective-permute-start | bytes 196616 | tf_op jit(solution)/shard_map/ppermute | solution.py:306
  76.2 3.1 %collective-permute-start.4 = (bf16[64,512]{1,0:T(8,128)(2,1)S(1)}, bf16[64,512]{1,0:T(8,128)(2,1)S(1)}, u32[]{:S(2)}, u32[]{:S(2)}) collective-permute-start(bf16[64,512]{1,0:T(8,128)(2,1)S(1)} %get-tuple-element.41), channel_id=1, source_target_pairs={{0,3},{1,2},{2,1},{3,0},{4,7},{5,6},{6,5},{7,4},{8,11},{9,10},{10,... | collective-permute-start | bytes 196616 | tf_op jit(solution)/shard_map/ppermute | solution.py:306
  79.4 1.2 %collective-permute-start.5 = (bf16[64,512]{1,0:T(8,128)(2,1)S(1)}, bf16[64,512]{1,0:T(8,128)(2,1)S(1)}, u32[]{:S(2)}, u32[]{:S(2)}) collective-permute-start(bf16[64,512]{1,0:T(8,128)(2,1)S(1)} %get-tuple-element.42), channel_id=1, source_target_pairs={{0,2},{1,3},{2,0},{3,1},{4,6},{5,7},{6,4},{7,5},{8,10},{9,11},{10,... | collective-permute-start | bytes 196616 | tf_op jit(solution)/shard_map/ppermute | solution.py:306
  80.6 1.0 %shard_map.162 = f32[64,512]{1,0:T(8,128)} custom-call(bf16[1024,128]{1,0:T(8,128)(2,1)S(1)} %bitcast.14, bf16[256,256]{1,0:T(8,128)(2,1)S(1)} %copy-done), custom_call_target="tpu_custom_call" | custom-call | tf_op jit(solution)/shard_map/pallas_call | solution.py:278
  81.6 0.0 collective-permute-done.3.came1_ref
  81.6 1.8 %collective-permute-done.4.came3_ref = bf16[64,512]{1,0:T(8,128)(2,1)S(1)} collective-permute-done((bf16[64,512]{1,0:T(8,128)(2,1)S(1)}, bf16[64,512]{1,0:T(8,128)(2,1)S(1)}, u32[]{:S(2)}, u32[]{:S(2)}) %collective-permute-start.4) | collective-permute-done | bytes 65568 | tf_op jit(solution)/shard_map/ppermute | solution.py:306
  83.3 5.4 %collective-permute-done.5.came2_ref = bf16[64,512]{1,0:T(8,128)(2,1)S(1)} collective-permute-done((bf16[64,512]{1,0:T(8,128)(2,1)S(1)}, bf16[64,512]{1,0:T(8,128)(2,1)S(1)}, u32[]{:S(2)}, u32[]{:S(2)}) %collective-permute-start.5) | collective-permute-done | bytes 65568 | tf_op jit(solution)/shard_map/ppermute | solution.py:306
  88.7 0.0 all-to-all-done.3
  88.7 0.7 shard_map.161
  (3 shorter events, 0.0 us)
Async XLA Ops:
  1.5 13.3 %collective-permute-start.2 = (bf16[128,512]{1,0:T(8,128)(2,1)S(1)}, bf16[128,512]{1,0:T(8,128)(2,1)S(1)}, u32[]{:S(2)}, u32[]{:S(2)}) collective-permute-start(bf16[128,512]{1,0:T(8,128)(2,1)S(1)} %shard_map.155.own_ref), channel_id=1, source_target_pairs={{0,2},{1,3},{2,0},{3,1},{4,6},{5,7},{6,4},{7,5},{8,10},{9,11},{10,... | collective-permute-start | bytes 393224 | tf_op jit(solution)/shard_map/ppermute | solution.py:306
  7.9 11.8 %collective-permute-start.1 = (bf16[128,512]{1,0:T(8,128)(2,1)S(1)}, bf16[128,512]{1,0:T(8,128)(2,1)S(1)}, u32[]{:S(2)}, u32[]{:S(2)}) collective-permute-start(bf16[128,512]{1,0:T(8,128)(2,1)S(1)} %shard_map.155.own_ref), channel_id=1, source_target_pairs={{0,3},{1,2},{2,1},{3,0},{4,7},{5,6},{6,5},{7,4},{8,11},{9,10},{10,... | collective-permute-start | bytes 393224 | tf_op jit(solution)/shard_map/ppermute | solution.py:306
  8.4 11.3 %collective-permute-start = (bf16[128,512]{1,0:T(8,128)(2,1)S(1)}, bf16[128,512]{1,0:T(8,128)(2,1)S(1)}, u32[]{:S(2)}, u32[]{:S(2)}) collective-permute-start(bf16[128,512]{1,0:T(8,128)(2,1)S(1)} %shard_map.155.own_ref), channel_id=1, source_target_pairs={{0,1},{1,0},{2,3},{3,2},{4,5},{5,4},{6,7},{7,6},{8,9},{9,8},{10,11... | collective-permute-start | bytes 393224 | tf_op jit(solution)/shard_map/ppermute | solution.py:306
  9.4 10.4 %copy-start = (bf16[256,256]{1,0:T(8,128)(2,1)S(1)}, bf16[256,256]{1,0:T(8,128)(2,1)}, u32[]{:S(2)}) copy-start(bf16[256,256]{1,0:T(8,128)(2,1)} %constant.20.clone.swap_ref.refs_1_) | copy-start | bytes 393220
  9.4 28.9 %copy-start.3 = (bf16[1024,256]{1,0:T(8,128)(2,1)S(1)}, bf16[1024,256]{1,0:T(8,128)(2,1)}, u32[]{:S(2)}) copy-start(bf16[1024,256]{1,0:T(8,128)(2,1)} %constant.16.clone.outer_ref) | copy-start | bytes 1572868
  19.7 18.6 %copy-start.1 = (bf16[512,512]{1,0:T(8,128)(2,1)S(1)}, bf16[512,512]{1,0:T(8,128)(2,1)}, u32[]{:S(2)}) copy-start(bf16[512,512]{1,0:T(8,128)(2,1)} %constant.18.clone.last_ref) | copy-start | bytes 1572868
  19.7 18.6 %copy-start.2 = (bf16[1024,256]{1,0:T(8,128)(2,1)S(1)}, bf16[1024,256]{1,0:T(8,128)(2,1)}, u32[]{:S(2)}) copy-start(bf16[1024,256]{1,0:T(8,128)(2,1)} %constant.17.clone.inner_ref) | copy-start | bytes 1572868
  20.3 18.0 %copy-start.4 = (bf16[128,128]{1,0:T(8,128)(2,1)S(1)}, bf16[128,128]{1,0:T(8,128)(2,1)}, u32[]{:S(2)}) copy-start(bf16[128,128]{1,0:T(8,128)(2,1)} %constant.21.clone.half_swap_ref.swap_ref) | copy-start | bytes 98308
  68.7 20.0 %all-to-all-start.3 = ((bf16[64,8,128]{2,1,0:T(8,128)(2,1)}), bf16[64,8,128]{2,1,0:T(8,128)(2,1)S(1)}, u32[]{:S(2)}, u32[]{:S(2)}) async-start(bf16[64,8,128]{2,1,0:T(8,128)(2,1)} %bitcast.9), calls=%async_computation.3 | async-start | bytes 262144 | tf_op jit(solution)/shard_map/all_to_all | solution.py:302
  74.0 7.6 %collective-permute-start.3 = (bf16[64,512]{1,0:T(8,128)(2,1)S(1)}, bf16[64,512]{1,0:T(8,128)(2,1)S(1)}, u32[]{:S(2)}, u32[]{:S(2)}) collective-permute-start(bf16[64,512]{1,0:T(8,128)(2,1)S(1)} %get-tuple-element.40), channel_id=1, source_target_pairs={{0,1},{1,0},{2,3},{3,2},{4,5},{5,4},{6,7},{7,6},{8,9},{9,8},{10,11... | collective-permute-start | bytes 196616 | tf_op jit(solution)/shard_map/ppermute | solution.py:306
  76.2 7.1 %collective-permute-start.4 = (bf16[64,512]{1,0:T(8,128)(2,1)S(1)}, bf16[64,512]{1,0:T(8,128)(2,1)S(1)}, u32[]{:S(2)}, u32[]{:S(2)}) collective-permute-start(bf16[64,512]{1,0:T(8,128)(2,1)S(1)} %get-tuple-element.41), channel_id=1, source_target_pairs={{0,3},{1,2},{2,1},{3,0},{4,7},{5,6},{6,5},{7,4},{8,11},{9,10},{10,... | collective-permute-start | bytes 196616 | tf_op jit(solution)/shard_map/ppermute | solution.py:306
  79.4 9.3 %collective-permute-start.5 = (bf16[64,512]{1,0:T(8,128)(2,1)S(1)}, bf16[64,512]{1,0:T(8,128)(2,1)S(1)}, u32[]{:S(2)}, u32[]{:S(2)}) collective-permute-start(bf16[64,512]{1,0:T(8,128)(2,1)S(1)} %get-tuple-element.42), channel_id=1, source_target_pairs={{0,2},{1,3},{2,0},{3,1},{4,6},{5,7},{6,4},{7,5},{8,10},{9,11},{10,... | collective-permute-start | bytes 196616 | tf_op jit(solution)/shard_map/ppermute | solution.py:306
